TPU v7x, 768 devices: a whole 4x8x12 slice. The times are simulated.
768 devices in a mesh: seq: 8 (over y), exp: 48 (over z, x), enc: 2 (over core).
Axes of the slice: x: 4, y: 8, z: 12, core: 2. Of those that a mesh axis runs over, the one named last changes fastest.
Arguments:
- patches: bfloat16 [48, 16, 68, 1152], P('exp', ('seq', 'enc')), may hold values from -6 to 6
- image_counts: int32 [48, 16], P('exp'), may hold values from 1 to 17, 256 in all within a row
- image_order: int32 [48, 16], P('exp'), may hold values from 0 to 15, each once within a row
- w_merge: bfloat16 [4608, 3456], P(None, ('seq', 'enc')), may hold values from -0.09375 to 0.09375
- w_proj_out: bfloat16 [8, 2, 216, 7168], P(None, 'enc', None, 'seq'), may hold values from -0.109375 to 0.109375
- routes: int32 [12288, 8], P(('exp', 'enc')), may hold values from 0 to 383, all different within a row; in each aligned block of 128 rows (0 to 127, 128 to 255, ...) at most 3 rows name the same one
- route_weight: float32 [12288, 8], P(('exp', 'enc')), may hold values from 0.2 to 1
- expert_place: int32 [384], replicated, may hold values from -1 to 47, as said below
- w_gate: bfloat16 [48, 7168, 1024], P('exp', None, 'seq'), may hold values from -0.0625 to 0.0625
- w_up: bfloat16 [48, 7168, 1024], P('exp', None, 'seq'), may hold values from -0.0625 to 0.0625
- w_down: bfloat16 [48, 1024, 7168], P('exp', 'seq'), may hold values from -0.1875 to 0.1875
Outputs:
- hidden_out: bfloat16 [12288, 7168], P(('exp', 'enc'), 'seq')
- expert_load: float32 [48, 2], P('exp', 'enc')
Inputs may be any that keep to these rules, and one draw needn't show every extreme that they name: `image_counts`: in each row the counts sum to 256 and the largest is exactly 17. `image_order`: each row is a permutation of 0 to 15. `routes`: each row names 8 different experts; among the 128 rows of one device no expert is named by more than 3 rows, a bound that some block reaches. `expert_place`: each of 0 to 47 appears exactly once; every other entry is -1.
All inputs are finite; a program needn't handle non-finite values.
Results may differ from a plain program's by a relative error of at most 0.014.
Values may be sent and summed in bfloat16 or wider, within the bound.
No kernel may reach another device: no remote copies, remote signals or barrier semaphores. Data moves between devices by JAX's collectives and lax.ppermute only.
A program may use at most 128 MiB of HBM per device.

v0:
```python
import jax
import jax.numpy as jnp
from jax import lax
from jax.sharding import PartitionSpec as P

D = 7168
ALL_EXPERTS = 384
TOP = 8
MERGE = 4
CAP = 3


def in_blocks(shard, dim, peers):
    before, after = (shard.shape[:dim], shard.shape[dim + 1 :])
    return jnp.moveaxis(shard.reshape(*before, peers, -1, *after), dim, 0)


def summed_on_arrival(shard, axis, dim):
    peers = lax.axis_size(axis)
    parts = lax.all_to_all(in_blocks(shard, dim, peers), axis, 0, 0, tiled=True)
    return jnp.sum(parts.astype(jnp.float32), axis=0)


def side_by_side(arrays, axis, split_dim, concat_dim, along):
    columns = [a.reshape(*a.shape[:along], -1) for a in arrays]
    both = jnp.concatenate(columns, axis=along)
    out, at, gathered = (
        lax.all_to_all(both, axis, split_axis=split_dim, concat_axis=concat_dim, tiled=True),
        0,
        [],
    )
    for a, column in zip(arrays, columns):
        slab = out[..., at : at + column.shape[along]]
        gathered.append(slab.reshape(*slab.shape[:along], *a.shape[along:]))
        at += column.shape[along]
    return tuple(gathered)


def sent_to_all(shard, axis):
    copies = jnp.broadcast_to(shard, (lax.axis_size(axis), *shard.shape))
    return lax.all_to_all(copies, axis, split_axis=0, concat_axis=0, tiled=True)


def in_order(parts, dim):
    parts = jnp.moveaxis(parts, 0, dim)
    dims = parts.shape
    return parts.reshape(*dims[:dim], dims[dim] * dims[dim + 1], *dims[dim + 2 :])


def gathered_copies(shard, axis, dim):
    parts = sent_to_all(shard, axis)
    return in_order(parts, dim)


def layer_norm(values):
    centre_mean = jnp.mean(values, axis=-1, keepdims=True)
    centred = values - centre_mean
    variance = jnp.mean(centred * centred, axis=-1, keepdims=True)
    return centred * lax.rsqrt(variance + 1e-06)


def sequence_rows(counts, order, seq_len, image_cap):
    shard_total = counts.shape[0]
    shard_ids = jnp.arange(shard_total, dtype=jnp.int32)
    picked = (order[:, None] == shard_ids[None, :]).astype(jnp.int32)
    ordered = jnp.sum(picked * counts[None, :], axis=1)
    run_ends = jnp.cumsum(ordered)
    run_starts = run_ends - ordered
    position = jnp.arange(seq_len, dtype=jnp.int32)
    image_slot = jnp.sum((position[:, None] >= run_ends[None, :]).astype(jnp.int32), axis=1)
    selected = (image_slot[:, None] == shard_ids[None, :]).astype(jnp.int32)
    shard_id = jnp.sum(selected * order[None, :], axis=1)
    first_row = jnp.sum(selected * run_starts[None, :], axis=1)
    return shard_id * image_cap + position - first_row


def slot_table(routes, weights, place, n_dest, cap):
    token_count, top_count = routes.shape
    target = jnp.take(place, routes.reshape(-1), axis=0)
    onehot = (target[:, None] == jnp.arange(n_dest, dtype=jnp.int32)[None, :]).astype(jnp.int32)
    rank_here = jnp.sum((jnp.cumsum(onehot, axis=0) - 1) * onehot, axis=1)
    slot_id = jnp.where(target >= 0, target * cap + rank_here, -1)
    matches = slot_id[None, :] == jnp.arange(n_dest * cap, dtype=jnp.int32)[:, None]
    token_of = jnp.arange(token_count * top_count, dtype=jnp.int32) // top_count
    slot_tok = jnp.sum(jnp.where(matches, token_of[None, :], 0), axis=1)
    live_slot = jnp.any(matches, axis=1)
    mixing = jnp.where(matches, weights.reshape(-1)[None, :], jnp.zeros((), weights.dtype))
    mixing = jnp.sum(mixing.reshape(n_dest * cap, token_count, top_count), axis=2)
    return (slot_tok, live_slot, mixing)


def shards(
    patches,
    image_counts,
    image_order,
    w_merge,
    w_proj_out,
    routes,
    route_weight,
    expert_place,
    w_gate,
    w_up,
    w_down,
):
    seq_count = lax.axis_size("seq")
    enc_count = lax.axis_size("enc")
    exp_count = lax.axis_size("exp")
    image_cap = patches.shape[2] // MERGE
    vit_width = patches.shape[3]
    token_count = routes.shape[0]
    seq_len = token_count * enc_count
    columns = w_proj_out.shape[3]
    unit_count = w_merge.shape[1]
    unit_block = w_proj_out.shape[2]
    piece = lax.all_gather(patches, ("seq", "enc"), axis=1, tiled=True)
    shard_count = piece.shape[1]
    normed = layer_norm(piece[0].astype(jnp.float32)).astype(jnp.bfloat16)
    merged = normed.reshape(shard_count * image_cap, MERGE * vit_width)
    inner_act = jax.nn.gelu(
        jnp.dot(merged, w_merge, preferred_element_type=jnp.float32), approximate=False
    )
    inner_all = inner_act.astype(jnp.bfloat16).reshape(1, shard_count, image_cap, unit_count)
    placed = jnp.take(
        inner_all.reshape(-1, unit_count),
        sequence_rows(image_counts[0], image_order[0], seq_len, image_cap),
        axis=0,
    )
    weight_rows = w_proj_out.reshape(seq_count * unit_block, columns)
    partial_out = jnp.dot(
        lax.all_gather(placed, "seq", axis=1, tiled=True),
        weight_rows,
        preferred_element_type=jnp.float32,
    )
    x_cols = summed_on_arrival(partial_out.astype(jnp.bfloat16), "enc", 0).astype(jnp.bfloat16)
    slot_tok, live_slot, mixing = slot_table(routes, route_weight, expert_place, exp_count, CAP)
    live_flags = live_slot.astype(jnp.bfloat16).reshape(exp_count, CAP)
    gate_w = w_gate[0]
    up_w = w_up[0]
    slot_rows = jnp.where(
        live_slot[:, None], jnp.take(x_cols, slot_tok, axis=0), jnp.zeros((), jnp.bfloat16)
    )
    arrived, flags_in = side_by_side(
        (slot_rows.reshape(exp_count, CAP, columns), live_flags), "exp", 0, 0, 2
    )
    piece = gathered_copies(arrived, "seq", 2)
    flattened = piece.reshape(exp_count * CAP, piece.shape[2])
    gate_sum = jnp.dot(flattened, gate_w, preferred_element_type=jnp.float32)
    up_sum = jnp.dot(flattened, up_w, preferred_element_type=jnp.float32)
    squares = jnp.sum(jnp.square(flattened.astype(jnp.float32)), axis=1)
    inv_rms = lax.rsqrt(squares / D + 1e-06)[:, None]
    hidden = (jax.nn.silu(gate_sum * inv_rms) * (up_sum * inv_rms)).astype(jnp.bfloat16)
    down_part = jnp.dot(hidden, w_down[0], preferred_element_type=jnp.float32)
    outputs = summed_on_arrival(down_part.astype(jnp.bfloat16), "seq", 1).astype(jnp.bfloat16)
    returned = lax.all_to_all(
        outputs.reshape(exp_count, CAP, columns), "exp", split_axis=0, concat_axis=0, tiled=True
    )
    combined = jnp.dot(
        mixing.T,
        returned.reshape(exp_count * CAP, columns).astype(jnp.float32),
        precision=lax.Precision.HIGHEST,
    )
    hidden_out = (x_cols.astype(jnp.float32) + combined).astype(jnp.bfloat16)
    expert_load = jnp.sum(flags_in.astype(jnp.float32)) * (
        ALL_EXPERTS / (exp_count * token_count * TOP)
    )
    return (hidden_out, expert_load.reshape(1, 1))


def solution(mesh):
    in_specs = (
        P("exp", ("seq", "enc"), None, None),
        P("exp", None),
        P("exp", None),
        P(None, ("seq", "enc")),
        P(None, "enc", None, "seq"),
        P(("exp", "enc"), None),
        P(("exp", "enc"), None),
        P(),
        P("exp", None, "seq"),
        P("exp", None, "seq"),
        P("exp", "seq", None),
    )
    out_specs = (P(("exp", "enc"), "seq"), P("exp", "enc"))
    return jax.shard_map(shards, mesh=mesh, in_specs=in_specs, out_specs=out_specs, check_vma=False)
```

profile of v0, /device:TPU:2, one launch (start us, length us, event | category | flops | bytes accessed | tf_op | source)
XLA Modules:
  0.0 324.6 jit_solution(13023961555795294974)
XLA Ops:
  7.2 0.7 all-gather.2.cloned.1.call-update
  7.9 0.9 copy.105
  9.2 6.9 %gather_fusion.1 = s32[1024]{0:T(1024)S(1)} fusion(s32[384]{0:T(512)S(1)} %copy-done.1, s32[1024]{0:T(1024)S(1)} %broadcast_clamp_fusion), kind=kCustom, calls=%fused_computation.1 | custom fusion | bytes 12288 | tf_op jit(solution)/shard_map/jit(_take)/gather | solution.py:79
  16.1 13.5 %reduce-window.18 = s32[48,8,128]{2,1,0:T(8,128)S(1)} reduce-window(s32[48,8,128]{2,1,0:T(8,128)S(1)} %fusion.36, s32[]{:T(128)} %constant.50.clone.1), window={size=1x1x128 pad=0_0x0_0x127_0}, to_apply=%region_8.9 | reduce-window | flops 6242304 | bytes 393220 | tf_op jit(solution)/shard_map/reduce-window.1
  29.7 0.1 copy.109
  30.2 0.2 fusion.23
  30.4 0.1 broadcast_in_dim.101
  30.5 0.2 select_reduce_fusion.4
  31.0 0.1 select_reduce_fusion
  31.2 0.2 reshape.335
  31.7 30.5 %all-gather.2.cloned.1.call-done = bf16[1,16,68,1152]{3,2,0,1:T(8,128)(2,1)} async-done(((bf16[1,1,68,1152]{3,2,0,1:T(8,128)(2,1)}), bf16[1,16,68,1152]{3,2,0,1:T(8,128)(2,1)}) %all-gather.2.cloned.1.call-update) | async-done | bytes 2506768 | tf_op jit(solution)/shard_map/all_gather | solution.py:115
  62.2 2.4 convert_reduce_fusion
  64.6 0.2 copy-done.2
  64.8 0.9 fusion.1
  65.7 2.7 mul.125
  68.4 4.5 %mul.126 = f32[272,4608]{1,0:T(8,128)} reshape(f32[16,68,1152]{2,1,0:T(8,128)} %mul.125) | data formatting | bytes 10027008 | tf_op jit(solution)/shard_map/mul | solution.py:59
  72.9 2.7 sub.50
  75.7 4.5 %sub.51 = f32[272,4608]{1,0:T(8,128)} reshape(f32[16,68,1152]{2,1,0:T(8,128)} %sub.50) | data formatting | bytes 10027008 | tf_op jit(solution)/shard_map/sub | solution.py:57
  80.2 4.5 %reshape.309 = f32[272,4608]{1,0:T(8,128)} reshape(bf16[1,16,68,1152]{3,2,0,1:T(8,128)(2,1)} %all-gather.2.cloned.1.call-done) | data formatting | bytes 7520256 | tf_op jit(solution)/shard_map/convert_element_type | solution.py:117
  84.7 7.4 %fusion.26 = bf16[272,216]{1,0:T(8,128)(2,1)S(1)} fusion(bf16[4608,216]{0,1:T(8,128)(2,1)} %param.14, f32[272,4608]{1,0:T(8,128)} %mul.126, f32[272,4608]{1,0:T(8,128)} %reshape.309, f32[272,4608]{1,0:T(8,128)} %sub.51), kind=kOutput, calls=%fused_computation.34 | convolution fusion | flops 549037440 | bytes 17148672 | tf_op jit(solution)/shard_map/dot_general | solution.py:120
  92.1 1.2 gather_fusion
  93.4 26.3 %all_gather.7 = bf16[256,1728]{0,1:T(8,128)(2,1)S(1)} all-gather(bf16[256,216]{0,1:T(8,128)(2,1)S(1)} %copy.104), channel_id=1, replica_groups=mesh['seq'=8,'exp'=48,'enc'=2] {'seq'}, dimensions={1}, use_global_device_ids=true | all-gather | bytes 995328 | tf_op jit(solution)/shard_map/all_gather | solution.py:130
  119.8 1.1 convolution_convert_fusion.1
  120.9 4.8 %all_to_all.25 = bf16[2,128,896]{2,1,0:T(8,128)(2,1)} all-to-all(bf16[2,128,896]{2,1,0:T(8,128)(2,1)S(1)} %bitcast.83), channel_id=1, replica_groups=mesh['seq'=8,'exp'=48,'enc'=2] {'enc'}, dimensions={0} | all-to-all | bytes 917504 | tf_op jit(solution)/shard_map/all_to_all | solution.py:20
  125.7 1.1 reduce_sum.138
  126.8 1.6 gather_fusion.2
  128.5 1.8 gather.23
  130.2 1.3 select_select_fusion
  131.5 0.2 pad_maximum_fusion
  131.7 34.1 %all_to_all.26 = bf16[48,3,897]{2,1,0:T(4,128)(2,1)S(1)} all-to-all(bf16[48,3,897]{2,1,0:T(4,128)(2,1)S(1)} %pad_maximum_fusion), channel_id=1, replica_groups=mesh['seq'=8,'exp'=48,'enc'=2] {'exp'}, dimensions={0} | all-to-all | bytes 516672 | tf_op jit(solution)/shard_map/all_to_all | solution.py:28
  166.0 0.6 copy-done.3
  166.6 0.2 broadcast_in_dim.108
  166.8 53.2 %all_to_all.27 = bf16[8,48,3,896]{3,1,2,0:T(8,128)(2,1)S(1)} all-to-all(bf16[8,48,3,896]{3,1,2,0:T(8,128)(2,1)S(1)} %broadcast_in_dim.108), channel_id=1, replica_groups=mesh['seq'=8,'exp'=48,'enc'=2] {'seq'}, dimensions={0} | all-to-all | bytes 4128768 | tf_op jit(solution)/shard_map/all_to_all | solution.py:41
  220.0 0.4 copy.114
  220.4 1.7 copy.119
  222.1 0.5 multiply_reduce_fusion
  222.9 2.8 fusion.9
  225.7 5.3 %convolution_convert_fusion = bf16[144,7168]{1,0:T(8,128)(2,1)} fusion(bf16[1,128,7168]{2,1,0:T(8,128)(2,1)} %param.21, bf16[144,7168]{1,0:T(8,128)(2,1)} %bitcast.77, bf16[1,7168,128]{2,1,0:T(8,128)(2,1)} %param.20, f32[144,128]{1,0:T(8,128)S(1)} %fusion.9, f32[144]{0:T(256)S(1)} %rsqrt.20), kind=kOutput, calls=%fused_computation.3 | convolution fusion | flops 529643520 | bytes 7873088 | tf_op jit(solution)/shard_map/dot_general | solution.py:152
  231.0 1.7 copy.122
  232.7 50.9 %all_to_all.28 = bf16[8,144,896]{2,1,0:T(8,128)(2,1)} all-to-all(bf16[8,144,896]{2,1,0:T(8,128)(2,1)S(1)} %bitcast.80), channel_id=1, replica_groups=mesh['seq'=8,'exp'=48,'enc'=2] {'seq'}, dimensions={0} | all-to-all | bytes 4128768 | tf_op jit(solution)/shard_map/all_to_all | solution.py:20
  283.6 2.7 reduce_sum.146
  286.3 1.8 reshape.306
  288.1 8.4 %all-to-all-start.4 = ((bf16[48,3,896]{2,1,0:T(4,128)(2,1)}), bf16[48,3,896]{2,1,0:T(4,128)(2,1)}, u32[]{:S(2)}, u32[]{:S(2)}) async-start(bf16[48,3,896]{2,1,0:T(4,128)(2,1)} %reshape.306), calls=%async_computation.4 | async-start | bytes 688128 | tf_op jit(solution)/shard_map/all_to_all | solution.py:154
  296.9 0.2 select_reduce_fusion.1
  297.1 1.5 convert_reduce_fusion.1
  299.2 13.5 %all-to-all-done.4 = bf16[48,3,896]{2,1,0:T(4,128)(2,1)} async-done(((bf16[48,3,896]{2,1,0:T(4,128)(2,1)}), bf16[48,3,896]{2,1,0:T(4,128)(2,1)}, u32[]{:S(2)}, u32[]{:S(2)}) %all-to-all-start.4) | async-done | bytes 258080 | tf_op jit(solution)/shard_map/all_to_all | solution.py:154
  312.6 1.9 reshape.307
  314.5 2.1 fusion.8
  (59 shorter events, 2.3 us)
Async XLA Ops:
  7.2 112.6 %copy-start = (bf16[8,1,216,896]{3,2,1,0:T(8,128)(2,1)S(1)}, bf16[8,1,216,896]{3,2,1,0:T(8,128)(2,1)}, u32[]{:S(2)}) copy-start(bf16[8,1,216,896]{3,2,1,0:T(8,128)(2,1)} %param.15) | copy-start | bytes 9289732
  7.2 2.0 copy-start.1
  7.2 55.0 %all-gather.2.cloned.1.call-start = ((), (), s32[]{:S(2)}) async-start(), calls=%async_computation.5 | async-start | bytes 2820096 | tf_op jit(solution)/shard_map/all_gather | solution.py:115
  9.2 21.3 %copy-start.6 = (s32[1,16]{1,0:T(1,128)S(1)}, s32[1,16]{1,0:T(1,128)}, u32[]{:S(2)}) copy-start(s32[1,16]{1,0:T(1,128)} %param.13) | copy-start | bytes 196
  9.2 21.3 %copy-start.7 = (s32[1,16]{1,0:T(1,128)S(1)}, s32[1,16]{1,0:T(1,128)}, u32[]{:S(2)}) copy-start(s32[1,16]{1,0:T(1,128)} %param.12) | copy-start | bytes 196
  62.2 2.5 copy-start.2
  165.9 0.7 copy-start.3
  283.6 13.2 %copy-start.4 = (s32[128,8]{0,1:T(8,128)S(1)}, s32[128,8]{0,1:T(8,128)}, u32[]{:S(2)}) copy-start(s32[128,8]{0,1:T(8,128)} %param.16) | copy-start | bytes 12292
  283.6 13.2 %copy-start.5 = (f32[128,8]{0,1:T(8,128)S(1)}, f32[128,8]{0,1:T(8,128)}, u32[]{:S(2)}) copy-start(f32[128,8]{0,1:T(8,128)} %param.17) | copy-start | bytes 12292
  288.1 24.5 %all-to-all-start.4 = ((bf16[48,3,896]{2,1,0:T(4,128)(2,1)}), bf16[48,3,896]{2,1,0:T(4,128)(2,1)}, u32[]{:S(2)}, u32[]{:S(2)}) async-start(bf16[48,3,896]{2,1,0:T(4,128)(2,1)} %reshape.306), calls=%async_computation.4 | async-start | bytes 688128 | tf_op jit(solution)/shard_map/all_to_all | solution.py:154
Sparse Core Ops, SparseCore 0:
  10.4 51.7 all-gather.1
where the time goes:
time: 325 us
  blocking collectives  169 us (52%)
  waiting for transfers between devices  44.6 us (14%)
  local copies, waits for them, and re-layouts  41.8 us (13%)
  other arithmetic  25.4 us (8%)
  matrix products  18.7 us (6%)
  between operations  16.2 us (5%)
  starting transfers between devices  8.47 us (3%)
    all_to_all x2, blocking collectives, summed_on_arrival(): parts = lax.all_to_all(in_blocks(shard, dim, peers), axis, 0, 0, tiled=True)  55.7 us
    all_to_all x1, blocking collectives, sent_to_all(): return lax.all_to_all(copies, axis, split_axis=0, concat_axis=0, tiled=True)  53.2 us
    all_to_all x1, blocking collectives, side_by_side(): lax.all_to_all(both, axis, split_axis=split_dim, concat_axis=concat_dim,...  34.1 us
    all_gather x1, waiting for transfers between devices, shards(): piece = lax.all_gather(patches, ('seq', 'enc'), axis=1, tiled=True)  30.5 us
    all_gather x1, blocking collectives, shards(): lax.all_gather(placed, 'seq', axis=1, tiled=True)  26.3 us
    another operation x4, other arithmetic  13.7 us
    all_to_all x1, waiting for transfers between devices, shards(): lax.all_to_all(outputs.reshape(exp_count, CAP, columns), 'exp', split_axi...  13.5 us
    all_to_all x1, starting transfers between devices, shards(): lax.all_to_all(outputs.reshape(exp_count, CAP, columns), 'exp', split_axi...  8.43 us
  transfers between devices with their start and end apart: 2, of which 2 were waited for; matrix products, arithmetic and copies ran while one was open for 8% of the time, Pallas kernels for 0%

commit v1 on v0

v1 whole, which is shorter than its diff:
```python
import jax
import jax.numpy as jnp
from jax import lax
from jax.sharding import PartitionSpec as P

D = 7168
ALL_EXPERTS = 384
TOP = 8
MERGE = 4
CAP = 3
MARK = 2.0**60
BF = jnp.bfloat16
F32 = jnp.float32


def layer_norm(values):
    centre_mean = jnp.mean(values, axis=-1, keepdims=True)
    centred = values - centre_mean
    variance = jnp.mean(centred * centred, axis=-1, keepdims=True)
    return centred * lax.rsqrt(variance + 1e-06)


def shift(arr, axis, step):
    n = lax.axis_size(axis)
    return lax.ppermute(arr, axis, [(i, (i + step) % n) for i in range(n)])


def swap_cores(arr):
    return lax.ppermute(arr, "enc", [(0, 1), (1, 0)])


def apart(arr):
    n = lax.axis_size("seq")
    pairs = [(i * 2, (i + 1) % n * 2) for i in range(n)]
    pairs += [(i * 2 + 1, (i - 1) % n * 2 + 1) for i in range(n)]
    return lax.ppermute(arr, ("seq", "enc"), pairs)


def dot(a, b):
    return jnp.dot(a, b, preferred_element_type=F32)


def unmix(rows, image_cap):
    full = image_cap - 1
    r = jnp.arange(rows + MERGE, dtype=jnp.int32)
    source = jnp.where(r < full * MERGE, (r % full) * MERGE + r // full, r)
    return (source[:, None] == jnp.arange(rows, dtype=jnp.int32)[None, :]).astype(BF)


def projector_rows(blocks, image_cap):
    full = image_cap - 1
    n, _, width = blocks.shape
    main = [blocks[:, m * full : (m + 1) * full].reshape(n * full, width) for m in range(MERGE)]
    last = [blocks[:, MERGE * full + m] for m in range(MERGE)]
    return jnp.concatenate([jnp.concatenate(main, 1), jnp.concatenate(last, 1)], 0)


def place_of_positions(counts, order, seq_len):
    shard_total = counts.shape[0]
    ids = jnp.arange(shard_total, dtype=jnp.int32)
    ordered = jnp.sum((order[:, None] == ids[None, :]) * counts[None, :], axis=1)
    ends = jnp.sum((ids[None, :] <= ids[:, None]) * ordered[None, :], axis=1)
    starts = ends - ordered
    p = jnp.arange(seq_len, dtype=jnp.int32)
    inside = (p[:, None] >= starts[None, :]) & (p[:, None] < ends[None, :])
    shard = jnp.sum(inside * order[None, :], axis=1)
    offset = p - jnp.sum(inside * starts[None, :], axis=1)
    return shard, offset


def slot_matrix(routes, weights, place, n_dest):
    tokens = routes.shape[0]
    slots = n_dest * CAP
    row = jnp.arange(slots, dtype=jnp.int32)
    numbers = jnp.arange(place.shape[0], dtype=jnp.int32)
    expert = jnp.sum(jnp.where(place[None, :] == (row // CAP)[:, None], numbers[None, :], 0), axis=1)
    match = routes.T[None, :, :] == expert[:, None, None]
    hit = jnp.any(match, axis=1)
    weight = jnp.sum(jnp.where(match, weights.T[None, :, :], 0.0), axis=1)
    t = jnp.arange(tokens, dtype=jnp.int32)
    before = dot(hit.astype(BF), (t[:, None] < t[None, :]).astype(BF))
    mine = hit & (before == (row % CAP).astype(F32)[:, None])
    return mine, jnp.where(mine, weight, 0.0)


def shards(
    patches,
    image_counts,
    image_order,
    w_merge,
    w_proj_out,
    routes,
    route_weight,
    expert_place,
    w_gate,
    w_up,
    w_down,
):
    n_seq = lax.axis_size("seq")
    enc_count = lax.axis_size("enc")
    exp_count = lax.axis_size("exp")
    s = lax.axis_index("seq")
    c = lax.axis_index("enc")
    image_cap = patches.shape[2] // MERGE
    tokens = routes.shape[0]
    seq_len = tokens * enc_count
    columns = w_proj_out.shape[3]
    unit_block = w_proj_out.shape[2]
    half_ring = n_seq // 2

    normed = layer_norm(patches[0, 0].astype(F32)).astype(BF)
    own = dot(unmix(normed.shape[0], image_cap), normed).astype(BF)[None]
    pair = jnp.concatenate([own, swap_cores(own)], 0)
    arrived, travelling = [pair], pair
    for k in range(1, half_ring + 1):
        if k == half_ring:
            travelling = travelling[:1]
        travelling = apart(travelling)
        arrived += [travelling, swap_cores(travelling)]
    cut = 5
    inners = []
    for group in (arrived[:cut], arrived[cut:]):
        rows = projector_rows(jnp.concatenate(group, 0), image_cap)
        inners.append(jax.nn.gelu(dot(rows, w_merge), approximate=False).astype(BF))
    inner = jnp.concatenate(inners, 0)

    shard, offset = place_of_positions(image_counts[0], image_order[0], seq_len)
    away = ((shard // enc_count - s) * (2 * c - 1)) % n_seq
    other = (shard % enc_count != c).astype(jnp.int32)
    near = jnp.where(away < half_ring, away, n_seq - away)
    spot = 2 + (near - 1) * 4 + jnp.where(away < half_ring, other, 3 - other)
    spot = jnp.where(away == 0, other, jnp.where(away == half_ring, 2 + 4 * (half_ring - 1) + other, spot))
    first = 2 + 4 * (cut // 2)
    full = image_cap - 1
    late = spot >= first
    n_group = jnp.where(late, n_seq * enc_count - first, first)
    base = jnp.where(late, first * image_cap, 0)
    inside = spot - jnp.where(late, first, 0)
    row = base + jnp.where(offset < full, inside * full + offset, n_group * full + inside)
    pick = (row[:, None] == jnp.arange(inner.shape[0], dtype=jnp.int32)[None, :]).astype(BF)
    placed = dot(pick, inner).astype(BF)

    units = lax.all_gather(placed, "seq", axis=1, tiled=True)
    partial_out = dot(units, w_proj_out.reshape(n_seq * unit_block, columns)).astype(BF)

    down_w = w_down[0]
    half_units = down_w.shape[0] // enc_count
    half = lax.dynamic_slice_in_dim(down_w, c * half_units, half_units, 0)
    half = jnp.moveaxis(half.reshape(half_units, n_seq, columns), 1, 0)
    half, partial_out = lax.optimization_barrier((half, partial_out))
    down_mine = lax.all_to_all(half, "seq", 0, 0, tiled=True)
    down_other = swap_cores(down_mine)
    down_cols = jnp.where(
        c == 0,
        jnp.concatenate([down_mine, down_other], 1),
        jnp.concatenate([down_other, down_mine], 1),
    ).reshape(-1, columns)

    halves = partial_out.reshape(enc_count, tokens, columns)
    keep = lax.dynamic_index_in_dim(halves, c, 0, keepdims=False)
    give = lax.dynamic_index_in_dim(halves, 1 - c, 0, keepdims=False)
    x_cols = (keep.astype(F32) + swap_cores(give).astype(F32)).astype(BF)

    mine, mixing = slot_matrix(routes, route_weight, expert_place, exp_count)
    slot_rows = dot(mine.astype(BF), x_cols)
    empty = ~jnp.any(mine, axis=1)
    mark_here = empty[:, None] & (jnp.arange(columns, dtype=jnp.int32) == 0)[None, :]
    slot_rows = jnp.where(mark_here, MARK, slot_rows).astype(BF)
    got = lax.all_to_all(slot_rows.reshape(exp_count, CAP, columns), "exp", 0, 0, tiled=True)
    got = got.reshape(exp_count * CAP, columns)
    live = got[:, 0].astype(F32) < MARK / 1024
    expert_load = jnp.sum(live.astype(F32)) * (ALL_EXPERTS / (exp_count * tokens * TOP))

    gate_w = w_gate[0].reshape(n_seq, columns, -1)
    up_w = w_up[0].reshape(n_seq, columns, -1)

    def terms(k, block):
        at = (s + k) % n_seq
        wide = block.astype(F32)
        return (
            dot(block, lax.dynamic_index_in_dim(gate_w, at, 0, keepdims=False)),
            dot(block, lax.dynamic_index_in_dim(up_w, at, 0, keepdims=False)),
            jnp.sum(wide * wide, axis=1, keepdims=True),
        )

    total = terms(0, got)
    right = left = got
    for k in range(1, half_ring):
        right, left = shift(right, "seq", 1), shift(left, "seq", -1)
        for step, block in ((-k, right), (k, left)):
            total = tuple(a + b for a, b in zip(total, terms(step, block)))
    cut_row = got.shape[0] // 2
    block = jnp.concatenate([shift(right[:cut_row], "seq", 1), shift(left[cut_row:], "seq", -1)], 0)
    gate_sum, up_sum, squares = (a + b for a, b in zip(total, terms(half_ring, block)))
    inv_rms = lax.rsqrt(squares / D + 1e-06)
    hidden = (jax.nn.silu(gate_sum * inv_rms) * (up_sum * inv_rms)).astype(BF)
    hidden_all = lax.all_gather(hidden, "seq", axis=1, tiled=True)
    outputs = dot(hidden_all, down_cols).astype(BF)

    returned = lax.all_to_all(outputs.reshape(exp_count, CAP, columns), "exp", 0, 0, tiled=True)
    combined = lax.dot_general(
        mixing,
        returned.reshape(exp_count * CAP, columns).astype(F32),
        (((0,), (0,)), ((), ())),
        precision=lax.Precision.HIGHEST,
    )
    hidden_out = (x_cols.astype(F32) + combined).astype(BF)
    return (hidden_out, expert_load.reshape(1, 1))


def solution(mesh):
    in_specs = (
        P("exp", ("seq", "enc"), None, None),
        P("exp", None),
        P("exp", None),
        P(None, ("seq", "enc")),
        P(None, "enc", None, "seq"),
        P(("exp", "enc"), None),
        P(("exp", "enc"), None),
        P(),
        P("exp", None, "seq"),
        P("exp", None, "seq"),
        P("exp", "seq", None),
    )
    out_specs = (P(("exp", "enc"), "seq"), P("exp", "enc"))
    return jax.shard_map(shards, mesh=mesh, in_specs=in_specs, out_specs=out_specs, check_vma=False)
```

time: 325 us -> 272 us (0.84)
  the two profiles are of different devices: /device:TPU:2 before, /device:TPU:8 now
where the time goes in v1:
time: 272 us; the launch traced here: 271 us
  waiting for transfers between devices  75.8 us (28%)
  starting transfers between devices  74.6 us (27%)
  blocking collectives  51.1 us (19%)
  matrix products  31.1 us (11%)
  local copies, waits for them, and re-layouts  21 us (8%)
  other arithmetic  13.9 us (5%)
  between operations  3.23 us (1%)
    dot_general x24, matrix products, dot(): return jnp.dot(a, b, preferred_element_type=F32)  28.8 us
    all_gather x1, blocking collectives, shards(): units = lax.all_gather(placed, 'seq', axis=1, tiled=True)  26.4 us
    all_gather x1, blocking collectives, shards(): hidden_all = lax.all_gather(hidden, 'seq', axis=1, tiled=True)  24.7 us
    ppermute x8, starting transfers between devices, shift(): return lax.ppermute(arr, axis, [(i, (i + step) % n) for i in range(n)])  24.7 us
    ppermute x4, waiting for transfers between devices, apart(): return lax.ppermute(arr, ('seq', 'enc'), pairs)  24.5 us
    all_to_all x1, waiting for transfers between devices, shards(): lax.all_to_all(slot_rows.reshape(exp_count, CAP, columns), 'exp', 0, 0, t...  18.1 us
    ppermute x8, waiting for transfers between devices, shift(): return lax.ppermute(arr, axis, [(i, (i + step) % n) for i in range(n)])  17.8 us
    ppermute x7, starting transfers between devices, swap_cores(): return lax.ppermute(arr, 'enc', [(0, 1), (1, 0)])  14.7 us
  transfers between devices with their start and end apart: 22, of which 10 were waited for; matrix products, arithmetic and copies ran while one was open for 18% of the time, Pallas kernels for 0%

profile of v1, /device:TPU:8, one launch (start us, length us, event | category | flops | bytes accessed | tf_op | source)
XLA Modules:
  0.0 270.7 jit_solution(25436509253005733)
XLA Ops:
  3.0 1.9 constant_dynamic-update-slice_fusion.5
  4.9 1.9 collective-permute-start
  8.2 2.2 constant_dynamic-slice_fusion
  10.8 2.2 copy.41
  13.3 3.5 %collective-permute-start.1 = (bf16[2,72,1152]{2,1,0:T(8,128)(2,1)S(1)}, bf16[2,72,1152]{2,1,0:T(8,128)(2,1)S(1)}, u32[]{:S(2)}, u32[]{:S(2)}) collective-permute-start(bf16[2,72,1152]{2,1,0:T(8,128)(2,1)S(1)} %pad_maximum_fusion), channel_id=1, source_target_pairs={{0,96},{96,192},{192,288},{288,384},{384,480},{480,576},{576,672},... | collective-permute-start | bytes 995336 | tf_op jit(solution)/shard_map/ppermute | solution.py:36
  17.0 12.8 %collective-permute-done.1 = bf16[2,72,1152]{2,1,0:T(8,128)(2,1)S(1)} collective-permute-done((bf16[2,72,1152]{2,1,0:T(8,128)(2,1)S(1)}, bf16[2,72,1152]{2,1,0:T(8,128)(2,1)S(1)}, u32[]{:S(2)}, u32[]{:S(2)}) %collective-permute-start.1) | collective-permute-done | bytes 331808 | tf_op jit(solution)/shard_map/ppermute | solution.py:36
  29.8 1.9 collective-permute-start.2
  31.7 1.9 collective-permute-start.3
  35.0 6.9 %collective-permute-done.3 = bf16[2,72,1152]{2,1,0:T(8,128)(2,1)S(1)} collective-permute-done((bf16[2,72,1152]{2,1,0:T(8,128)(2,1)S(1)}, bf16[2,72,1152]{2,1,0:T(8,128)(2,1)S(1)}, u32[]{:S(2)}, u32[]{:S(2)}) %collective-permute-start.3) | collective-permute-done | bytes 331808 | tf_op jit(solution)/shard_map/ppermute | solution.py:36
  41.9 1.9 collective-permute-start.4
  43.8 1.9 collective-permute-start.5
  48.1 1.6 fusion.164
  49.6 1.5 fusion.165
  51.2 2.9 %collective-permute-done.5 = bf16[2,72,1152]{2,1,0:T(8,128)(2,1)S(1)} collective-permute-done((bf16[2,72,1152]{2,1,0:T(8,128)(2,1)S(1)}, bf16[2,72,1152]{2,1,0:T(8,128)(2,1)S(1)}, u32[]{:S(2)}, u32[]{:S(2)}) %collective-permute-start.5) | collective-permute-done | bytes 331808 | tf_op jit(solution)/shard_map/ppermute | solution.py:36
  54.1 1.9 collective-permute-start.7
  56.0 3.3 %collective-permute-start.6 = (bf16[2,72,1152]{2,1,0:T(8,128)(2,1)S(1)}, bf16[2,72,1152]{2,1,0:T(8,128)(2,1)S(1)}, u32[]{:S(2)}, u32[]{:S(2)}) collective-permute-start(bf16[2,72,1152]{2,1,0:T(8,128)(2,1)S(1)} %collective-permute-done.5), channel_id=1, source_target_pairs={{0,1},{1,0},{2,3},{3,2},{4,5},{5,4},{6,7},{7,6},{8,9},{9,8},{10,11... | collective-permute-start | bytes 995336 | tf_op jit(solution)/shard_map/ppermute | solution.py:29
  60.5 2.0 collective-permute-done.7
  62.5 1.9 collective-permute-start.8
  67.3 26.4 %all_gather.6 = bf16[256,1728]{0,1:T(8,128)(2,1)S(1)} all-gather(bf16[256,216]{0,1:T(8,128)(2,1)S(1)} %convolution_convert_fusion.3), channel_id=1, replica_groups=mesh['seq'=8,'exp'=48,'enc'=2] {'seq'}, dimensions={1}, use_global_device_ids=true | all-gather | bytes 995328 | tf_op jit(solution)/shard_map/all_gather | solution.py:143
  95.7 1.9 collective-permute-start.9
  99.4 1.9 fusion.17
  101.3 1.8 reshape.269
  103.0 11.6 %all-to-all-start = ((bf16[48,3,896]{2,1,0:T(4,128)(2,1)}), bf16[48,3,896]{2,1,0:T(4,128)(2,1)S(1)}, u32[]{:S(2)}, u32[]{:S(2)}) async-start(bf16[48,3,896]{2,1,0:T(4,128)(2,1)} %reshape.269), calls=%async_computation | async-start | bytes 688128 | tf_op jit(solution)/shard_map/all_to_all | solution.py:169
  114.7 2.3 copy.30
  117.0 18.1 %all-to-all-done = bf16[48,3,896]{2,1,0:T(4,128)(2,1)S(1)} async-done(((bf16[48,3,896]{2,1,0:T(4,128)(2,1)}), bf16[48,3,896]{2,1,0:T(4,128)(2,1)S(1)}, u32[]{:S(2)}, u32[]{:S(2)}) %all-to-all-start) | async-done | bytes 258080 | tf_op jit(solution)/shard_map/all_to_all | solution.py:169
  135.1 8.0 %all-to-all-start.1 = ((bf16[8,64,896]{2,1,0:T(8,128)(2,1)}), bf16[8,64,896]{2,1,0:T(8,128)(2,1)}, u32[]{:S(2)}, u32[]{:S(2)}) async-start(bf16[8,64,896]{2,1,0:T(8,128)(2,1)} %copy.30), calls=%async_computation.1 | async-start | bytes 1835008 | tf_op jit(solution)/shard_map/all_to_all | solution.py:151
  144.0 3.4 %collective-permute-start.10 = (bf16[144,896]{1,0:T(8,128)(2,1)}, bf16[144,896]{1,0:T(8,128)(2,1)}, u32[]{:S(2)}, u32[]{:S(2)}) collective-permute-start(bf16[144,896]{1,0:T(8,128)(2,1)} %reshape.270), channel_id=1, source_target_pairs={{0,96},{96,192},{192,288},{288,384},{384,480},{480,576},{576,672},... | collective-permute-start | bytes 774152 | tf_op jit(solution)/shard_map/ppermute | solution.py:25
  147.3 2.5 collective-permute-start.11
  151.5 1.3 fusion.72
  152.8 15.6 %collective-permute-done.11 = bf16[144,896]{1,0:T(8,128)(2,1)} collective-permute-done((bf16[144,896]{1,0:T(8,128)(2,1)}, bf16[144,896]{1,0:T(8,128)(2,1)}, u32[]{:S(2)}, u32[]{:S(2)}) %collective-permute-start.11) | collective-permute-done | bytes 258080 | tf_op jit(solution)/shard_map/ppermute | solution.py:25
  168.4 2.5 collective-permute-start.13
  170.8 3.4 %collective-permute-start.12 = (bf16[144,896]{1,0:T(8,128)(2,1)}, bf16[144,896]{1,0:T(8,128)(2,1)}, u32[]{:S(2)}, u32[]{:S(2)}) collective-permute-start(bf16[144,896]{1,0:T(8,128)(2,1)} %collective-permute-done.10), channel_id=1, source_target_pairs={{0,96},{96,192},{192,288},{288,384},{384,480},{480,576},{576,672},... | collective-permute-start | bytes 774152 | tf_op jit(solution)/shard_map/ppermute | solution.py:25
  174.2 1.3 convolution_add_fusion.3
  175.5 1.3 convolution_add_fusion.7
  181.6 4.0 %collective-permute-start.14 = (bf16[144,896]{1,0:T(8,128)(2,1)}, bf16[144,896]{1,0:T(8,128)(2,1)}, u32[]{:S(2)}, u32[]{:S(2)}) collective-permute-start(bf16[144,896]{1,0:T(8,128)(2,1)} %collective-permute-done.12), channel_id=1, source_target_pairs={{0,96},{96,192},{192,288},{288,384},{384,480},{480,576},{576,672},... | collective-permute-start | bytes 774152 | tf_op jit(solution)/shard_map/ppermute | solution.py:25
  185.6 1.9 collective-permute-start.15
  191.3 1.3 fusion.22
  194.9 1.9 collective-permute-start.18
  197.8 5.1 %collective-permute-start.16 = (bf16[72,896]{1,0:T(8,128)(2,1)S(1)}, bf16[72,896]{1,0:T(8,128)(2,1)S(1)}, u32[]{:S(2)}, u32[]{:S(2)}) collective-permute-start(bf16[72,896]{1,0:T(8,128)(2,1)S(1)} %slice.97), channel_id=1, source_target_pairs={{0,96},{96,192},{192,288},{288,384},{384,480},{480,576},{576,672},... | collective-permute-start | bytes 387080 | tf_op jit(solution)/shard_map/ppermute | solution.py:25
  203.0 1.9 collective-permute-start.17
  208.5 2.2 collective-permute-done.17
  213.2 1.3 fusion.21
  214.5 1.3 multiply_convert_fusion
  215.9 24.7 %all_gather.7 = bf16[144,1024]{1,0:T(8,128)(2,1)S(1)} all-gather(bf16[144,128]{1,0:T(8,128)(2,1)S(1)} %multiply_convert_fusion), channel_id=1, replica_groups=mesh['seq'=8,'exp'=48,'enc'=2] {'seq'}, dimensions={1}, use_global_device_ids=true | all-gather | bytes 331776 | tf_op jit(solution)/shard_map/all_gather | solution.py:197
  240.5 2.0 maximum_select_fusion
  244.0 6.4 %all-to-all-start.2 = ((bf16[48,3,896]{2,1,0:T(4,128)(2,1)}), bf16[48,3,896]{2,1,0:T(4,128)(2,1)S(1)}, u32[]{:S(2)}, u32[]{:S(2)}) async-start(bf16[48,3,896]{2,1,0:T(4,128)(2,1)} %reshape.271), calls=%async_computation.2 | async-start | bytes 688128 | tf_op jit(solution)/shard_map/all_to_all | solution.py:200
  252.8 13.6 %all-to-all-done.2 = bf16[48,3,896]{2,1,0:T(4,128)(2,1)S(1)} async-done(((bf16[48,3,896]{2,1,0:T(4,128)(2,1)}), bf16[48,3,896]{2,1,0:T(4,128)(2,1)S(1)}, u32[]{:S(2)}, u32[]{:S(2)}) %all-to-all-start.2) | async-done | bytes 258080 | tf_op jit(solution)/shard_map/all_to_all | solution.py:200
  267.2 2.3 add_convert_fusion
  (106 shorter events, 40.4 us)
Async XLA Ops:
  0.6 93.1 %copy-start = (bf16[8,1,216,896]{3,2,1,0:T(8,128)(2,1)S(1)}, bf16[8,1,216,896]{3,2,1,0:T(8,128)(2,1)}, u32[]{:S(2)}) copy-start(bf16[8,1,216,896]{3,2,1,0:T(8,128)(2,1)} %param.15) | copy-start | bytes 9289732
  0.6 9.8 %copy-start.7 = (s32[384]{0:T(512)S(1)}, s32[384]{0:T(512)}, u32[]{:S(2)}) copy-start(s32[384]{0:T(512)} %param.18) | copy-start | bytes 4612
  4.9 8.4 %collective-permute-start = (bf16[1,72,1152]{2,1,0:T(8,128)(2,1)S(1)}, bf16[1,72,1152]{2,1,0:T(8,128)(2,1)S(1)}, u32[]{:S(2)}, u32[]{:S(2)}) collective-permute-start(bf16[1,72,1152]{2,1,0:T(8,128)(2,1)S(1)} %get-tuple-element.27), channel_id=1, source_target_pairs={{0,1},{1,0},{2,3},{3,2},{4,5},{5,4},{6,7},{7,6},{8,9},{9,8},{10,11... | collective-permute-start | bytes 497672 | tf_op jit(solution)/shard_map/ppermute | solution.py:29
  8.2 4.8 %copy-start.2 = (s32[128,8]{0,1:T(8,128)S(1)}, s32[128,8]{0,1:T(8,128)}, u32[]{:S(2)}) copy-start(s32[128,8]{0,1:T(8,128)} %param.16) | copy-start | bytes 12292
  8.2 8.6 %copy-start.9 = (s32[1,16]{1,0:T(1,128)S(1)}, s32[1,16]{1,0:T(1,128)}, u32[]{:S(2)}) copy-start(s32[1,16]{1,0:T(1,128)} %param.13) | copy-start | bytes 196
  10.6 35.9 %copy-start.4 = (s32[144]{0:T(256)}, s32[144]{0:T(256)S(1)}, u32[]{:S(2)}) copy-start(s32[144]{0:T(256)S(1)} %select_reduce_fusion) | copy-start | bytes 1732
  13.3 16.4 %collective-permute-start.1 = (bf16[2,72,1152]{2,1,0:T(8,128)(2,1)S(1)}, bf16[2,72,1152]{2,1,0:T(8,128)(2,1)S(1)}, u32[]{:S(2)}, u32[]{:S(2)}) collective-permute-start(bf16[2,72,1152]{2,1,0:T(8,128)(2,1)S(1)} %pad_maximum_fusion), channel_id=1, source_target_pairs={{0,96},{96,192},{192,288},{288,384},{384,480},{480,576},{576,672},... | collective-permute-start | bytes 995336 | tf_op jit(solution)/shard_map/ppermute | solution.py:36
  29.8 16.0 %collective-permute-start.2 = (bf16[2,72,1152]{2,1,0:T(8,128)(2,1)S(1)}, bf16[2,72,1152]{2,1,0:T(8,128)(2,1)S(1)}, u32[]{:S(2)}, u32[]{:S(2)}) collective-permute-start(bf16[2,72,1152]{2,1,0:T(8,128)(2,1)S(1)} %collective-permute-done.1), channel_id=1, source_target_pairs={{0,1},{1,0},{2,3},{3,2},{4,5},{5,4},{6,7},{7,6},{8,9},{9,8},{10,11... | collective-permute-start | bytes 995336 | tf_op jit(solution)/shard_map/ppermute | solution.py:29
  31.7 10.2 %collective-permute-start.3 = (bf16[2,72,1152]{2,1,0:T(8,128)(2,1)S(1)}, bf16[2,72,1152]{2,1,0:T(8,128)(2,1)S(1)}, u32[]{:S(2)}, u32[]{:S(2)}) collective-permute-start(bf16[2,72,1152]{2,1,0:T(8,128)(2,1)S(1)} %collective-permute-done.1), channel_id=1, source_target_pairs={{0,96},{96,192},{192,288},{288,384},{384,480},{480,576},{576,672},... | collective-permute-start | bytes 995336 | tf_op jit(solution)/shard_map/ppermute | solution.py:36
  41.9 5.4 %collective-permute-start.4 = (bf16[2,72,1152]{2,1,0:T(8,128)(2,1)S(1)}, bf16[2,72,1152]{2,1,0:T(8,128)(2,1)S(1)}, u32[]{:S(2)}, u32[]{:S(2)}) collective-permute-start(bf16[2,72,1152]{2,1,0:T(8,128)(2,1)S(1)} %collective-permute-done.3), channel_id=1, source_target_pairs={{0,1},{1,0},{2,3},{3,2},{4,5},{5,4},{6,7},{7,6},{8,9},{9,8},{10,11... | collective-permute-start | bytes 995336 | tf_op jit(solution)/shard_map/ppermute | solution.py:29
  43.8 10.2 %collective-permute-start.5 = (bf16[2,72,1152]{2,1,0:T(8,128)(2,1)S(1)}, bf16[2,72,1152]{2,1,0:T(8,128)(2,1)S(1)}, u32[]{:S(2)}, u32[]{:S(2)}) collective-permute-start(bf16[2,72,1152]{2,1,0:T(8,128)(2,1)S(1)} %collective-permute-done.3), channel_id=1, source_target_pairs={{0,96},{96,192},{192,288},{288,384},{384,480},{480,576},{576,672},... | collective-permute-start | bytes 995336 | tf_op jit(solution)/shard_map/ppermute | solution.py:36
  48.1 11.3 %copy-start.10 = (bf16[4608,216]{0,1:T(8,128)(2,1)S(1)}, bf16[4608,216]{0,1:T(8,128)(2,1)}, u32[]{:S(2)}) copy-start(bf16[4608,216]{0,1:T(8,128)(2,1)} %param.14) | copy-start | bytes 5971972
  54.1 8.4 %collective-permute-start.7 = (bf16[1,72,1152]{2,1,0:T(8,128)(2,1)S(1)}, bf16[1,72,1152]{2,1,0:T(8,128)(2,1)S(1)}, u32[]{:S(2)}, u32[]{:S(2)}) collective-permute-start(bf16[1,72,1152]{2,1,0:T(8,128)(2,1)S(1)} %slice.88), channel_id=1, source_target_pairs={{0,96},{96,192},{192,288},{288,384},{384,480},{480,576},{576,672},... | collective-permute-start | bytes 497672 | tf_op jit(solution)/shard_map/ppermute | solution.py:36
  56.0 8.4 %collective-permute-start.6 = (bf16[2,72,1152]{2,1,0:T(8,128)(2,1)S(1)}, bf16[2,72,1152]{2,1,0:T(8,128)(2,1)S(1)}, u32[]{:S(2)}, u32[]{:S(2)}) collective-permute-start(bf16[2,72,1152]{2,1,0:T(8,128)(2,1)S(1)} %collective-permute-done.5), channel_id=1, source_target_pairs={{0,1},{1,0},{2,3},{3,2},{4,5},{5,4},{6,7},{7,6},{8,9},{9,8},{10,11... | collective-permute-start | bytes 995336 | tf_op jit(solution)/shard_map/ppermute | solution.py:29
  62.5 3.3 %collective-permute-start.8 = (bf16[1,72,1152]{2,1,0:T(8,128)(2,1)S(1)}, bf16[1,72,1152]{2,1,0:T(8,128)(2,1)S(1)}, u32[]{:S(2)}, u32[]{:S(2)}) collective-permute-start(bf16[1,72,1152]{2,1,0:T(8,128)(2,1)S(1)} %collective-permute-done.7), channel_id=1, source_target_pairs={{0,1},{1,0},{2,3},{3,2},{4,5},{5,4},{6,7},{7,6},{8,9},{9,8},{10,11... | collective-permute-start | bytes 497672 | tf_op jit(solution)/shard_map/ppermute | solution.py:29
  93.7 3.9 %copy-start.8 = (f32[144]{0:T(256)S(1)}, f32[144]{0:T(256)}, u32[]{:S(2)}) copy-start(f32[144]{0:T(256)} %get-tuple-element.29) | copy-start | bytes 1732
  94.9 8.2 %copy-start.1 = (bf16[256,896]{1,0:T(8,128)(2,1)}, bf16[256,896]{1,0:T(8,128)(2,1)S(1)}, u32[]{:S(2)}) copy-start(bf16[256,896]{1,0:T(8,128)(2,1)S(1)} %convolution_convert_fusion.1) | copy-start | bytes 1376260
  95.7 3.7 %collective-permute-start.9 = (bf16[128,896]{1,0:T(8,128)(2,1)}, bf16[128,896]{1,0:T(8,128)(2,1)}, u32[]{:S(2)}, u32[]{:S(2)}) collective-permute-start(bf16[128,896]{1,0:T(8,128)(2,1)} %dynamic-slice_bitcast_fusion), channel_id=1, source_target_pairs={{0,1},{1,0},{2,3},{3,2},{4,5},{5,4},{6,7},{7,6},{8,9},{9,8},{10,11... | collective-permute-start | bytes 688136 | tf_op jit(solution)/shard_map/ppermute | solution.py:29
  103.0 32.0 %all-to-all-start = ((bf16[48,3,896]{2,1,0:T(4,128)(2,1)}), bf16[48,3,896]{2,1,0:T(4,128)(2,1)S(1)}, u32[]{:S(2)}, u32[]{:S(2)}) async-start(bf16[48,3,896]{2,1,0:T(4,128)(2,1)} %reshape.269), calls=%async_computation | async-start | bytes 688128 | tf_op jit(solution)/shard_map/all_to_all | solution.py:169
  135.1 59.8 %all-to-all-start.1 = ((bf16[8,64,896]{2,1,0:T(8,128)(2,1)}), bf16[8,64,896]{2,1,0:T(8,128)(2,1)}, u32[]{:S(2)}, u32[]{:S(2)}) async-start(bf16[8,64,896]{2,1,0:T(8,128)(2,1)} %copy.30), calls=%async_computation.1 | async-start | bytes 1835008 | tf_op jit(solution)/shard_map/all_to_all | solution.py:151
  144.0 26.9 %collective-permute-start.10 = (bf16[144,896]{1,0:T(8,128)(2,1)}, bf16[144,896]{1,0:T(8,128)(2,1)}, u32[]{:S(2)}, u32[]{:S(2)}) collective-permute-start(bf16[144,896]{1,0:T(8,128)(2,1)} %reshape.270), channel_id=1, source_target_pairs={{0,96},{96,192},{192,288},{288,384},{384,480},{480,576},{576,672},... | collective-permute-start | bytes 774152 | tf_op jit(solution)/shard_map/ppermute | solution.py:25
  147.3 21.0 %collective-permute-start.11 = (bf16[144,896]{1,0:T(8,128)(2,1)}, bf16[144,896]{1,0:T(8,128)(2,1)}, u32[]{:S(2)}, u32[]{:S(2)}) collective-permute-start(bf16[144,896]{1,0:T(8,128)(2,1)} %reshape.270), channel_id=1, source_target_pairs={{0,672},{96,0},{192,96},{288,192},{384,288},{480,384},{576,480},{6... | collective-permute-start | bytes 774152 | tf_op jit(solution)/shard_map/ppermute | solution.py:25
  168.4 17.3 %collective-permute-start.13 = (bf16[144,896]{1,0:T(8,128)(2,1)}, bf16[144,896]{1,0:T(8,128)(2,1)}, u32[]{:S(2)}, u32[]{:S(2)}) collective-permute-start(bf16[144,896]{1,0:T(8,128)(2,1)} %collective-permute-done.11), channel_id=1, source_target_pairs={{0,672},{96,0},{192,96},{288,192},{384,288},{480,384},{576,480},{6... | collective-permute-start | bytes 774152 | tf_op jit(solution)/shard_map/ppermute | solution.py:25
  170.8 10.7 %collective-permute-start.12 = (bf16[144,896]{1,0:T(8,128)(2,1)}, bf16[144,896]{1,0:T(8,128)(2,1)}, u32[]{:S(2)}, u32[]{:S(2)}) collective-permute-start(bf16[144,896]{1,0:T(8,128)(2,1)} %collective-permute-done.10), channel_id=1, source_target_pairs={{0,96},{96,192},{192,288},{288,384},{384,480},{480,576},{576,672},... | collective-permute-start | bytes 774152 | tf_op jit(solution)/shard_map/ppermute | solution.py:25
  181.6 15.3 %collective-permute-start.14 = (bf16[144,896]{1,0:T(8,128)(2,1)}, bf16[144,896]{1,0:T(8,128)(2,1)}, u32[]{:S(2)}, u32[]{:S(2)}) collective-permute-start(bf16[144,896]{1,0:T(8,128)(2,1)} %collective-permute-done.12), channel_id=1, source_target_pairs={{0,96},{96,192},{192,288},{288,384},{384,480},{480,576},{576,672},... | collective-permute-start | bytes 774152 | tf_op jit(solution)/shard_map/ppermute | solution.py:25
  185.6 17.3 %collective-permute-start.15 = (bf16[144,896]{1,0:T(8,128)(2,1)}, bf16[144,896]{1,0:T(8,128)(2,1)S(1)}, u32[]{:S(2)}, u32[]{:S(2)}) collective-permute-start(bf16[144,896]{1,0:T(8,128)(2,1)} %collective-permute-done.13), channel_id=1, source_target_pairs={{0,672},{96,0},{192,96},{288,192},{384,288},{480,384},{576,480},{6... | collective-permute-start | bytes 774152 | tf_op jit(solution)/shard_map/ppermute | solution.py:25
  194.9 45.6 %collective-permute-start.18 = (bf16[8,64,896]{2,1,0:T(8,128)(2,1)}, bf16[8,64,896]{2,1,0:T(8,128)(2,1)S(1)}, u32[]{:S(2)}, u32[]{:S(2)}) collective-permute-start(bf16[8,64,896]{2,1,0:T(8,128)(2,1)} %all-to-all-done.1), channel_id=1, source_target_pairs={{0,1},{1,0},{2,3},{3,2},{4,5},{5,4},{6,7},{7,6},{8,9},{9,8},{10,11... | collective-permute-start | bytes 2752520 | tf_op jit(solution)/shard_map/ppermute | solution.py:29
  197.8 10.7 %collective-permute-start.16 = (bf16[72,896]{1,0:T(8,128)(2,1)S(1)}, bf16[72,896]{1,0:T(8,128)(2,1)S(1)}, u32[]{:S(2)}, u32[]{:S(2)}) collective-permute-start(bf16[72,896]{1,0:T(8,128)(2,1)S(1)} %slice.97), channel_id=1, source_target_pairs={{0,96},{96,192},{192,288},{288,384},{384,480},{480,576},{576,672},... | collective-permute-start | bytes 387080 | tf_op jit(solution)/shard_map/ppermute | solution.py:25
  203.0 7.7 %collective-permute-start.17 = (bf16[72,896]{1,0:T(8,128)(2,1)S(1)}, bf16[72,896]{1,0:T(8,128)(2,1)S(1)}, u32[]{:S(2)}, u32[]{:S(2)}) collective-permute-start(bf16[72,896]{1,0:T(8,128)(2,1)S(1)} %slice.98), channel_id=1, source_target_pairs={{0,672},{96,0},{192,96},{288,192},{384,288},{480,384},{576,480},{6... | collective-permute-start | bytes 387080 | tf_op jit(solution)/shard_map/ppermute | solution.py:25
  242.6 7.7 %copy-start.3 = (s32[128,8]{0,1:T(8,128)S(1)}, s32[128,8]{0,1:T(8,128)}, u32[]{:S(2)}) copy-start(s32[128,8]{0,1:T(8,128)} %param.16) | copy-start | bytes 12292
  242.6 7.7 %copy-start.5 = (s32[144]{0:T(256)S(1)}, s32[144]{0:T(256)}, u32[]{:S(2)}) copy-start(s32[144]{0:T(256)} %copy-done.4) | copy-start | bytes 1732
  242.6 7.7 %copy-start.6 = (f32[128,8]{0,1:T(8,128)S(1)}, f32[128,8]{0,1:T(8,128)}, u32[]{:S(2)}) copy-start(f32[128,8]{0,1:T(8,128)} %param.17) | copy-start | bytes 12292
  244.0 22.4 %all-to-all-start.2 = ((bf16[48,3,896]{2,1,0:T(4,128)(2,1)}), bf16[48,3,896]{2,1,0:T(4,128)(2,1)S(1)}, u32[]{:S(2)}, u32[]{:S(2)}) async-start(bf16[48,3,896]{2,1,0:T(4,128)(2,1)} %reshape.271), calls=%async_computation.2 | async-start | bytes 688128 | tf_op jit(solution)/shard_map/all_to_all | solution.py:200

commit v2 on v1

--- a/solution.py
+++ b/solution.py
@@ -1,6 +1,10 @@
+import functools
+
 import jax
 import jax.numpy as jnp
 from jax import lax
+from jax.experimental import pallas as pl
+from jax.experimental.pallas import tpu as pltpu
 from jax.sharding import PartitionSpec as P
 
 D = 7168
@@ -29,15 +33,143 @@
     return lax.ppermute(arr, "enc", [(0, 1), (1, 0)])
 
 
-def apart(arr):
+def apart(arr, k):
     n = lax.axis_size("seq")
-    pairs = [(i * 2, (i + 1) % n * 2) for i in range(n)]
-    pairs += [(i * 2 + 1, (i - 1) % n * 2 + 1) for i in range(n)]
+    pairs = [(i * 2, (i + k) % n * 2) for i in range(n)]
+    pairs += [(i * 2 + 1, (i - k) % n * 2 + 1) for i in range(n)]
     return lax.ppermute(arr, ("seq", "enc"), pairs)
 
 
 def dot(a, b):
     return jnp.dot(a, b, preferred_element_type=F32)
+
+
+def whole(shape):
+    return pl.BlockSpec(shape, lambda i, at: (0,) * len(shape))
+
+
+def multiplied(x, gate_ref, up_ref):
+    wide = x.astype(F32)
+    lanes = gate_ref.shape[1]
+    squares = sum(jnp.square(wide[:, k : k + lanes]) for k in range(0, wide.shape[1], lanes))
+    return dot(x, gate_ref[...]), dot(x, up_ref[...]), squares
+
+
+def absorb_kernel(n, more, at_ref, *refs):
+    blocks, gates, ups = refs[:n], refs[n : 2 * n], refs[2 * n : 3 * n]
+    terms = [multiplied(b[...], g, u) for b, g, u in zip(blocks, gates, ups)]
+    lanes = gates[0].shape[1]
+    for i in range(3):
+        total = terms[0][i]
+        for term in terms[1:]:
+            total = total + term[i]
+        if more:
+            total = total + refs[3 * n][:, i * lanes : (i + 1) * lanes]
+        refs[-1][:, i * lanes : (i + 1) * lanes] = total
+
+
+def weight_block(rows, lanes, j):
+    return pl.BlockSpec((rows, lanes), lambda i, at: (at[j], 0))
+
+
+def absorb(at, blocks, w_gate, w_up, total):
+    n, (rows, columns), lanes = len(blocks), blocks[0].shape, w_gate.shape[1]
+    more = [] if total is None else [total]
+    weights = [weight_block(columns, lanes, j) for j in range(n)]
+    return pl.pallas_call(
+        functools.partial(absorb_kernel, n, bool(more)),
+        out_shape=jax.ShapeDtypeStruct((rows, 3 * lanes), F32),
+        grid_spec=pltpu.PrefetchScalarGridSpec(
+            num_scalar_prefetch=1,
+            grid=(1,),
+            in_specs=[whole((rows, columns))] * n + weights + weights + [whole(m.shape) for m in more],
+            out_specs=whole((rows, 3 * lanes)),
+        ),
+        cost_estimate=pl.CostEstimate(
+            flops=n * 4 * rows * columns * lanes,
+            bytes_accessed=n * columns * (rows + 2 * lanes) * 2,
+            transcendentals=0,
+        ),
+        name="absorb",
+    )(at, *blocks, *[w_gate] * n, *[w_up] * n, *more)
+
+
+def finish_kernel(at_ref, upper_ref, lower_ref, gate_ref, up_ref, total_ref, out_ref):
+    start, lanes = 0, gate_ref.shape[1]
+    for ref in (upper_ref, lower_ref):
+        rows = slice(start, start + ref.shape[0])
+        gate, up, squares = multiplied(ref[...], gate_ref, up_ref)
+        squares = squares + total_ref[rows, 2 * lanes :]
+        inv_rms = lax.rsqrt(jnp.sum(squares, axis=1, keepdims=True) / D + 1e-06)
+        gate = (gate + total_ref[rows, :lanes]) * inv_rms
+        up = (up + total_ref[rows, lanes : 2 * lanes]) * inv_rms
+        hidden = (gate / (1.0 + jnp.exp(-gate)) * up).astype(BF)
+        for k in range(out_ref.shape[0]):
+            out_ref[k, rows, :] = hidden
+        start += ref.shape[0]
+
+
+def finish(at, upper, lower, w_gate, w_up, total, copies):
+    rows, columns, lanes = total.shape[0], upper.shape[1], w_gate.shape[1]
+    weight = weight_block(columns, lanes, 0)
+    return pl.pallas_call(
+        finish_kernel,
+        out_shape=jax.ShapeDtypeStruct((copies, rows, lanes), BF),
+        grid_spec=pltpu.PrefetchScalarGridSpec(
+            num_scalar_prefetch=1,
+            grid=(1,),
+            in_specs=[whole(upper.shape), whole(lower.shape), weight, weight, whole(total.shape)],
+            out_specs=whole((copies, rows, lanes)),
+        ),
+        cost_estimate=pl.CostEstimate(
+            flops=4 * rows * columns * lanes,
+            bytes_accessed=columns * (rows + 2 * lanes) * 2,
+            transcendentals=rows * lanes,
+        ),
+        name="finish",
+    )(at, upper, lower, w_gate, w_up, total)
+
+
+def down_kernel(hops, at_ref, hidden_ref, own_ref, mine_ref, other_ref, out_ref, far_ref, total_ref):
+    units = own_ref.shape[0]
+    half = units // 2
+    c = at_ref[2 * hops + 2]
+    far_ref[pl.ds(pl.multiple_of(c * half, half), half), :] = mine_ref[hops * units :, :]
+    far_ref[pl.ds(pl.multiple_of((1 - c) * half, half), half), :] = other_ref[hops * units :, :]
+    total_ref[...] = dot(hidden_ref[at_ref[0]], own_ref[...])
+    for side, ref in enumerate((mine_ref, other_ref)):
+        for k in range(hops):
+            block = hidden_ref[at_ref[1 + side * hops + k]]
+            total_ref[...] += dot(block, ref[k * units : (k + 1) * units, :])
+    total = total_ref[...] + dot(hidden_ref[at_ref[2 * hops + 1]], far_ref[...])
+    out_ref[...] = total.astype(out_ref.dtype)
+
+
+def down(at, hidden, w_down, mine, other, hops):
+    _, rows, units = hidden.shape
+    columns = mine.shape[1]
+    return pl.pallas_call(
+        functools.partial(down_kernel, hops),
+        out_shape=jax.ShapeDtypeStruct((rows, columns), BF),
+        grid_spec=pltpu.PrefetchScalarGridSpec(
+            num_scalar_prefetch=1,
+            grid=(1,),
+            in_specs=[
+                whole(hidden.shape),
+                pl.BlockSpec((units, columns), lambda i, at: (0, at[0])),
+                whole(mine.shape),
+                whole(other.shape),
+            ],
+            out_specs=whole((rows, columns)),
+            scratch_shapes=[pltpu.VMEM((units, columns), BF), pltpu.VMEM((rows, columns), F32)],
+        ),
+        cost_estimate=pl.CostEstimate(
+            flops=2 * hidden.size * columns,
+            bytes_accessed=2 * (hidden.size + 2 * mine.size + units * columns),
+            transcendentals=0,
+        ),
+        name="down",
+    )(at, hidden, w_down, mine, other)
 
 
 def unmix(rows, image_cap):
@@ -83,7 +215,7 @@
     return mine, jnp.where(mine, weight, 0.0)
 
 
-def shards(
+def layer(
     patches,
     image_counts,
     image_order,
@@ -111,51 +243,58 @@
     normed = layer_norm(patches[0, 0].astype(F32)).astype(BF)
     own = dot(unmix(normed.shape[0], image_cap), normed).astype(BF)[None]
     pair = jnp.concatenate([own, swap_cores(own)], 0)
-    arrived, travelling = [pair], pair
-    for k in range(1, half_ring + 1):
-        if k == half_ring:
-            travelling = travelling[:1]
-        travelling = apart(travelling)
-        arrived += [travelling, swap_cores(travelling)]
-    cut = 5
+    hops = [pair]
+    for _ in range(half_ring):
+        hops.append(apart(hops[-1], 1))
+    near = jnp.concatenate(hops[1:half_ring], 0)
+    near_other = swap_cores(near)
+    groups = (jnp.concatenate([pair, near], 0), near_other, hops[half_ring])
     inners = []
-    for group in (arrived[:cut], arrived[cut:]):
-        rows = projector_rows(jnp.concatenate(group, 0), image_cap)
+    for group in groups:
+        rows = projector_rows(group, image_cap)
         inners.append(jax.nn.gelu(dot(rows, w_merge), approximate=False).astype(BF))
     inner = jnp.concatenate(inners, 0)
 
     shard, offset = place_of_positions(image_counts[0], image_order[0], seq_len)
     away = ((shard // enc_count - s) * (2 * c - 1)) % n_seq
     other = (shard % enc_count != c).astype(jnp.int32)
-    near = jnp.where(away < half_ring, away, n_seq - away)
-    spot = 2 + (near - 1) * 4 + jnp.where(away < half_ring, other, 3 - other)
-    spot = jnp.where(away == 0, other, jnp.where(away == half_ring, 2 + 4 * (half_ring - 1) + other, spot))
-    first = 2 + 4 * (cut // 2)
+    base = jnp.zeros_like(shard)
+    inside, size = 2 * away + other, jnp.full_like(shard, groups[0].shape[0])
+    mirrored = away > half_ring
+    inside = jnp.where(mirrored, 2 * (n_seq - away - 1) + 1 - other, inside)
+    size = jnp.where(mirrored, groups[1].shape[0], size)
+    base = jnp.where(mirrored, groups[0].shape[0] * image_cap, base)
+    opposite = away == half_ring
+    inside = jnp.where(opposite, other, inside)
+    size = jnp.where(opposite, groups[2].shape[0], size)
+    base = jnp.where(opposite, (groups[0].shape[0] + groups[1].shape[0]) * image_cap, base)
     full = image_cap - 1
-    late = spot >= first
-    n_group = jnp.where(late, n_seq * enc_count - first, first)
-    base = jnp.where(late, first * image_cap, 0)
-    inside = spot - jnp.where(late, first, 0)
-    row = base + jnp.where(offset < full, inside * full + offset, n_group * full + inside)
+    row = base + jnp.where(offset < full, inside * full + offset, size * full + inside)
     pick = (row[:, None] == jnp.arange(inner.shape[0], dtype=jnp.int32)[None, :]).astype(BF)
     placed = dot(pick, inner).astype(BF)
 
+    down_w = w_down[0]
+    unit_rows = down_w.shape[0]
+    toward = 1 - 2 * c
+
+    def columns_of(device):
+        return lax.dynamic_slice_in_dim(down_w, device % n_seq * columns, columns, 1)
+
+    def after(arr, gate):
+        return lax.optimization_barrier((arr, gate))[0]
+
+    fetched = []
+    for k in range(1, half_ring + 1):
+        block = columns_of(s + toward * k)
+        if k == half_ring:
+            block = lax.dynamic_slice_in_dim(block, c * (unit_rows // 2), unit_rows // 2, 0)
+        fetched.append(apart(after(block, inners[0] if k < half_ring - 1 else placed), k))
+
     units = lax.all_gather(placed, "seq", axis=1, tiled=True)
     partial_out = dot(units, w_proj_out.reshape(n_seq * unit_block, columns)).astype(BF)
 
-    down_w = w_down[0]
-    half_units = down_w.shape[0] // enc_count
-    half = lax.dynamic_slice_in_dim(down_w, c * half_units, half_units, 0)
-    half = jnp.moveaxis(half.reshape(half_units, n_seq, columns), 1, 0)
-    half, partial_out = lax.optimization_barrier((half, partial_out))
-    down_mine = lax.all_to_all(half, "seq", 0, 0, tiled=True)
-    down_other = swap_cores(down_mine)
-    down_cols = jnp.where(
-        c == 0,
-        jnp.concatenate([down_mine, down_other], 1),
-        jnp.concatenate([down_other, down_mine], 1),
-    ).reshape(-1, columns)
-
+    mine_side = jnp.concatenate(fetched, 0)
+    other_side = swap_cores(mine_side)
     halves = partial_out.reshape(enc_count, tokens, columns)
     keep = lax.dynamic_index_in_dim(halves, c, 0, keepdims=False)
     give = lax.dynamic_index_in_dim(halves, 1 - c, 0, keepdims=False)
@@ -171,31 +310,26 @@
     live = got[:, 0].astype(F32) < MARK / 1024
     expert_load = jnp.sum(live.astype(F32)) * (ALL_EXPERTS / (exp_count * tokens * TOP))
 
-    gate_w = w_gate[0].reshape(n_seq, columns, -1)
-    up_w = w_up[0].reshape(n_seq, columns, -1)
-
-    def terms(k, block):
-        at = (s + k) % n_seq
-        wide = block.astype(F32)
-        return (
-            dot(block, lax.dynamic_index_in_dim(gate_w, at, 0, keepdims=False)),
-            dot(block, lax.dynamic_index_in_dim(up_w, at, 0, keepdims=False)),
-            jnp.sum(wide * wide, axis=1, keepdims=True),
-        )
-
-    total = terms(0, got)
+    def sources(*offsets):
+        return jnp.stack([(s + k) % n_seq for k in offsets]).astype(jnp.int32)
+
+    total = absorb(sources(0), (got,), w_gate[0], w_up[0], None)
     right = left = got
     for k in range(1, half_ring):
-        right, left = shift(right, "seq", 1), shift(left, "seq", -1)
-        for step, block in ((-k, right), (k, left)):
-            total = tuple(a + b for a, b in zip(total, terms(step, block)))
-    cut_row = got.shape[0] // 2
-    block = jnp.concatenate([shift(right[:cut_row], "seq", 1), shift(left[cut_row:], "seq", -1)], 0)
-    gate_sum, up_sum, squares = (a + b for a, b in zip(total, terms(half_ring, block)))
-    inv_rms = lax.rsqrt(squares / D + 1e-06)
-    hidden = (jax.nn.silu(gate_sum * inv_rms) * (up_sum * inv_rms)).astype(BF)
-    hidden_all = lax.all_gather(hidden, "seq", axis=1, tiled=True)
-    outputs = dot(hidden_all, down_cols).astype(BF)
+        left = shift(left, "seq", -1)
+        right = shift(right, "seq", 1)
+        total = absorb(sources(-k, k), (right, left), w_gate[0], w_up[0], total)
+    cut_row = (got.shape[0] // 2 + 15) // 16 * 16
+    lower = shift(left[cut_row:], "seq", -1)
+    upper = shift(right[:cut_row], "seq", 1)
+    hidden = finish(sources(half_ring), upper, lower, w_gate[0], w_up[0], total, n_seq)
+    hidden = lax.all_to_all(hidden, "seq", 0, 0, tiled=True)
+    hops_near = range(1, half_ring)
+    at = jnp.concatenate([
+        sources(0, *[-toward * k for k in hops_near], *[toward * k for k in hops_near], half_ring),
+        c.astype(jnp.int32)[None],
+    ])
+    outputs = down(at, hidden, down_w, mine_side, other_side, half_ring - 1)
 
     returned = lax.all_to_all(outputs.reshape(exp_count, CAP, columns), "exp", 0, 0, tiled=True)
     combined = lax.dot_general(
@@ -223,4 +357,4 @@
         P("exp", "seq", None),
     )
     out_specs = (P(("exp", "enc"), "seq"), P("exp", "enc"))
-    return jax.shard_map(shards, mesh=mesh, in_specs=in_specs, out_specs=out_specs, check_vma=False)
+    return jax.shard_map(layer, mesh=mesh, in_specs=in_specs, out_specs=out_specs, check_vma=False)

time: 272 us -> 257 us (0.945)
  the two profiles are of different devices: /device:TPU:8 before, /device:TPU:2 now
where the time goes in v2:
time: 257 us; the launch traced here: 256 us
  starting transfers between devices  88.6 us (34%)
  waiting for transfers between devices  74.3 us (29%)
  blocking collectives  27.3 us (11%)
  local copies, waits for them, and re-layouts  22.9 us (9%)
  Pallas kernels  18.3 us (7%)
  matrix products  11.1 us (4%)
  other arithmetic  10 us (4%)
  between operations  3.08 us (1%)
    ppermute x8, waiting for transfers between devices, apart(): return lax.ppermute(arr, ('seq', 'enc'), pairs)  27.4 us
    all_gather x1, blocking collectives, layer(): units = lax.all_gather(placed, 'seq', axis=1, tiled=True)  27.3 us
    ppermute x8, starting transfers between devices, shift(): return lax.ppermute(arr, axis, [(i, (i + step) % n) for i in range(n)])  26.1 us
    ppermute x8, starting transfers between devices, apart(): return lax.ppermute(arr, ('seq', 'enc'), pairs)  25.5 us
    all_to_all x1, waiting for transfers between devices, layer(): lax.all_to_all(slot_rows.reshape(exp_count, CAP, columns), 'exp', 0, 0, t...  19.2 us
    all_to_all x1, starting transfers between devices, layer(): lax.all_to_all(slot_rows.reshape(exp_count, CAP, columns), 'exp', 0, 0, t...  18.5 us
    all_to_all x1, waiting for transfers between devices, layer(): lax.all_to_all(outputs.reshape(exp_count, CAP, columns), 'exp', 0, 0, til...  13.8 us
    pallas_call x4, Pallas kernels, absorb(): pl.pallas_call(functools.partial(absorb_kernel, n, bool(more)), out_shape...  12.1 us
  transfers between devices with their start and end apart: 23, of which 12 were waited for; matrix products, arithmetic and copies ran while one was open for 9% of the time, Pallas kernels for 6%

profile of v2, /device:TPU:2, one launch (start us, length us, event | category | flops | bytes accessed | tf_op | source)
XLA Modules:
  0.0 255.6 jit_solution(4463358097626466354)
XLA Ops:
  3.0 1.9 constant_dynamic-update-slice_fusion.4
  4.9 1.9 collective-permute-start
  9.3 3.5 %collective-permute-start.1 = (bf16[2,72,1152]{2,1,0:T(8,128)(2,1)S(1)}, bf16[2,72,1152]{2,1,0:T(8,128)(2,1)S(1)}, u32[]{:S(2)}, u32[]{:S(2)}) collective-permute-start(bf16[2,72,1152]{2,1,0:T(8,128)(2,1)S(1)} %pad_maximum_fusion.1), channel_id=1, source_target_pairs={{0,96},{96,192},{192,288},{288,384},{384,480},{480,576},{576,672},... | collective-permute-start | bytes 995336 | tf_op jit(solution)/shard_map/ppermute | solution.py:40
  13.6 6.2 %collective-permute-done.1 = bf16[2,72,1152]{2,1,0:T(8,128)(2,1)S(1)} collective-permute-done((bf16[2,72,1152]{2,1,0:T(8,128)(2,1)S(1)}, bf16[2,72,1152]{2,1,0:T(8,128)(2,1)S(1)}, u32[]{:S(2)}, u32[]{:S(2)}) %collective-permute-start.1) | collective-permute-done | bytes 331808 | tf_op jit(solution)/shard_map/ppermute | solution.py:40
  19.8 2.0 collective-permute-start.2
  23.4 6.6 %collective-permute-done.2 = bf16[2,72,1152]{2,1,0:T(8,128)(2,1)S(1)} collective-permute-done((bf16[2,72,1152]{2,1,0:T(8,128)(2,1)S(1)}, bf16[2,72,1152]{2,1,0:T(8,128)(2,1)S(1)}, u32[]{:S(2)}, u32[]{:S(2)}) %collective-permute-start.2) | collective-permute-done | bytes 331808 | tf_op jit(solution)/shard_map/ppermute | solution.py:40
  30.0 1.9 collective-permute-start.3
  33.4 6.8 %collective-permute-done.3 = bf16[2,72,1152]{2,1,0:T(8,128)(2,1)S(1)} collective-permute-done((bf16[2,72,1152]{2,1,0:T(8,128)(2,1)S(1)}, bf16[2,72,1152]{2,1,0:T(8,128)(2,1)S(1)}, u32[]{:S(2)}, u32[]{:S(2)}) %collective-permute-start.3) | collective-permute-done | bytes 331808 | tf_op jit(solution)/shard_map/ppermute | solution.py:40
  41.0 1.4 fusion.126
  42.3 1.5 fusion.125
  44.0 1.9 collective-permute-start.4
  45.9 1.9 collective-permute-start.5
  48.9 7.2 %collective-permute-done.5 = bf16[2,72,1152]{2,1,0:T(8,128)(2,1)S(1)} collective-permute-done((bf16[2,72,1152]{2,1,0:T(8,128)(2,1)S(1)}, bf16[2,72,1152]{2,1,0:T(8,128)(2,1)S(1)}, u32[]{:S(2)}, u32[]{:S(2)}) %collective-permute-start.5) | collective-permute-done | bytes 331808 | tf_op jit(solution)/shard_map/ppermute | solution.py:40
  58.6 27.3 %all_gather.3 = bf16[256,1728]{0,1:T(8,128)(2,1)S(1)} all-gather(bf16[256,216]{0,1:T(8,128)(2,1)S(1)} %convolution_convert_fusion.2), channel_id=1, replica_groups=mesh['seq'=8,'exp'=48,'enc'=2] {'seq'}, dimensions={1}, use_global_device_ids=true | all-gather | bytes 995328 | tf_op jit(solution)/shard_map/all_gather | solution.py:293
  87.9 1.9 collective-permute-start.6
  91.6 1.9 fusion.17
  93.5 1.8 reshape.234
  95.3 18.5 %all-to-all-start = ((bf16[48,3,896]{2,1,0:T(4,128)(2,1)}), bf16[48,3,896]{2,1,0:T(4,128)(2,1)S(1)}, u32[]{:S(2)}, u32[]{:S(2)}) async-start(bf16[48,3,896]{2,1,0:T(4,128)(2,1)} %reshape.234), calls=%async_computation | async-start | bytes 688128 | tf_op jit(solution)/shard_map/all_to_all | solution.py:308
  113.8 19.2 %all-to-all-done = bf16[48,3,896]{2,1,0:T(4,128)(2,1)S(1)} async-done(((bf16[48,3,896]{2,1,0:T(4,128)(2,1)}), bf16[48,3,896]{2,1,0:T(4,128)(2,1)S(1)}, u32[]{:S(2)}, u32[]{:S(2)}) %all-to-all-start) | async-done | bytes 258080 | tf_op jit(solution)/shard_map/all_to_all | solution.py:308
  133.9 2.0 collective-permute-start.11
  135.9 3.9 %collective-permute-start.7 = (bf16[144,896]{1,0:T(8,128)(2,1)}, bf16[144,896]{1,0:T(8,128)(2,1)}, u32[]{:S(2)}, u32[]{:S(2)}) collective-permute-start(bf16[144,896]{1,0:T(8,128)(2,1)} %reshape.235.refs_0_), channel_id=1, source_target_pairs={{0,96},{96,192},{192,288},{288,384},{384,480},{480,576},{576,672},... | collective-permute-start | bytes 774152 | tf_op jit(solution)/shard_map/ppermute | solution.py:29
  139.8 2.0 dynamic-slice_bitcast_fusion
  141.8 3.0 %collective-permute-start.15 = (bf16[128,896]{1,0:T(8,128)(2,1)}, bf16[128,896]{1,0:T(8,128)(2,1)}, u32[]{:S(2)}, u32[]{:S(2)}) collective-permute-start(bf16[128,896]{1,0:T(8,128)(2,1)} %get-tuple-element.6), channel_id=1, source_target_pairs={{0,96},{96,192},{192,288},{288,384},{384,480},{480,576},{576,672},... | collective-permute-start | bytes 688136 | tf_op jit(solution)/shard_map/ppermute | solution.py:40
  144.8 4.8 %collective-permute-start.16 = (bf16[128,896]{1,0:T(8,128)(2,1)}, bf16[128,896]{1,0:T(8,128)(2,1)S(1)}, u32[]{:S(2)}, u32[]{:S(2)}) collective-permute-start(bf16[128,896]{1,0:T(8,128)(2,1)} %get-tuple-element.7), channel_id=1, source_target_pairs={{0,192},{96,288},{192,384},{288,480},{384,576},{480,672},{576,0},{... | collective-permute-start | bytes 688136 | tf_op jit(solution)/shard_map/ppermute | solution.py:40
  150.7 3.4 %collective-permute-start.17 = (bf16[128,896]{1,0:T(8,128)(2,1)}, bf16[128,896]{1,0:T(8,128)(2,1)S(1)}, u32[]{:S(2)}, u32[]{:S(2)}) collective-permute-start(bf16[128,896]{1,0:T(8,128)(2,1)} %get-tuple-element.8), channel_id=1, source_target_pairs={{0,288},{96,384},{192,480},{288,576},{384,672},{480,0},{576,96},{6... | collective-permute-start | bytes 688136 | tf_op jit(solution)/shard_map/ppermute | solution.py:40
  154.1 4.3 %collective-permute-start.12 = (bf16[144,896]{1,0:T(8,128)(2,1)S(1)}, bf16[144,896]{1,0:T(8,128)(2,1)}, u32[]{:S(2)}, u32[]{:S(2)}) collective-permute-start(bf16[144,896]{1,0:T(8,128)(2,1)S(1)} %collective-permute-done.11.refs_1_), channel_id=1, source_target_pairs={{0,672},{96,0},{192,96},{288,192},{384,288},{480,384},{576,480},{6... | collective-permute-start | bytes 774152 | tf_op jit(solution)/shard_map/ppermute | solution.py:29
  158.4 1.9 collective-permute-start.8
  160.4 1.6 constant_dynamic-update-slice_fusion.8
  162.7 5.0 %collective-permute-start.18 = (bf16[64,896]{1,0:T(8,128)(2,1)S(1)}, bf16[64,896]{1,0:T(8,128)(2,1)S(1)}, u32[]{:S(2)}, u32[]{:S(2)}) collective-permute-start(bf16[64,896]{1,0:T(8,128)(2,1)S(1)} %dynamic-slice_bitcast_fusion.4), channel_id=1, source_target_pairs={{0,384},{96,480},{192,576},{288,672},{384,0},{480,96},{576,192},{6... | collective-permute-start | bytes 344072 | tf_op jit(solution)/shard_map/ppermute | solution.py:40
  168.7 4.2 %collective-permute-start.13 = (bf16[144,896]{1,0:T(8,128)(2,1)}, bf16[144,896]{1,0:T(8,128)(2,1)}, u32[]{:S(2)}, u32[]{:S(2)}) collective-permute-start(bf16[144,896]{1,0:T(8,128)(2,1)} %collective-permute-done.12.refs_1_), channel_id=1, source_target_pairs={{0,672},{96,0},{192,96},{288,192},{384,288},{480,384},{576,480},{6... | collective-permute-start | bytes 774152 | tf_op jit(solution)/shard_map/ppermute | solution.py:29
  173.6 2.8 %collective-permute-start.9 = (bf16[144,896]{1,0:T(8,128)(2,1)}, bf16[144,896]{1,0:T(8,128)(2,1)S(1)}, u32[]{:S(2)}, u32[]{:S(2)}) collective-permute-start(bf16[144,896]{1,0:T(8,128)(2,1)} %collective-permute-done.8.refs_0_), channel_id=1, source_target_pairs={{0,96},{96,192},{192,288},{288,384},{384,480},{480,576},{576,672},... | collective-permute-start | bytes 774152 | tf_op jit(solution)/shard_map/ppermute | solution.py:29
  177.4 1.9 collective-permute-start.19
  180.7 2.5 collective-permute-done.9.refs_0_
  183.2 1.9 collective-permute-start.10
  185.2 1.5 slice.133
  186.7 5.1 %collective-permute-start.14 = (bf16[64,896]{1,0:T(8,128)(2,1)}, bf16[64,896]{1,0:T(8,128)(2,1)}, u32[]{:S(2)}, u32[]{:S(2)}) collective-permute-start(bf16[64,896]{1,0:T(8,128)(2,1)} %slice.133), channel_id=1, source_target_pairs={{0,672},{96,0},{192,96},{288,192},{384,288},{480,384},{576,480},{6... | collective-permute-start | bytes 344072 | tf_op jit(solution)/shard_map/ppermute | solution.py:29
  192.5 2.2 absorb.4.refs_6_
  194.6 3.3 %absorb.5.refs_6_ = f32[144,384]{1,0:T(8,128)} custom-call(s32[2]{0:T(128)} %pad_add_fusion.2.at_ref, bf16[144,896]{1,0:T(8,128)(2,1)} %collective-permute-done.7.refs_0_, bf16[144,896]{1,0:T(8,128)(2,1)} %copy-done.4, bf16[7168,128]{1,0:T(8,128)(2,1)} %bitcast.104, bf16[7168,128]{1,0:T(8,128)(2,1)} %bitcast.105, bf16[7168,128]{1,0:T(8,128)(2,1)} %bitcast.112, ...), custom_call_target="tpu_custom_call" | custom-call | flops 132120576 | bytes 1433600 | tf_op jit(solution)/shard_map/absorb/pallas_call | solution.py:79
  198.0 3.3 %absorb.6.refs_6_ = f32[144,384]{1,0:T(8,128)} custom-call(s32[2]{0:T(128)} %pad_add_fusion.1.at_ref, bf16[144,896]{1,0:T(8,128)(2,1)} %collective-permute-done.8.refs_0_, bf16[144,896]{1,0:T(8,128)(2,1)} %collective-permute-done.12.refs_1_, bf16[7168,128]{1,0:T(8,128)(2,1)} %bitcast.106, bf16[7168,128]{1,0:T(8,128)(2,1)} %bitcast.107, ...), custom_call_target="tpu_custom_call" | custom-call | flops 132120576 | bytes 1433600 | tf_op jit(solution)/shard_map/absorb/pallas_call | solution.py:79
  201.3 3.3 %absorb.7.total_ref = f32[144,384]{1,0:T(8,128)} custom-call(s32[2]{0:T(128)} %pad_add_fusion.at_ref, bf16[144,896]{1,0:T(8,128)(2,1)} %copy-done.2, bf16[144,896]{1,0:T(8,128)(2,1)} %collective-permute-done.13.refs_1_, bf16[7168,128]{1,0:T(8,128)(2,1)} %bitcast.108, bf16[7168,128]{1,0:T(8,128)(2,1)} %bitcast.109, bf16[7168,128]{1,0:T(8,128)(2,1)} %bitcast.116, ...), custom_call_target="tpu_custom_call" | custom-call | flops 132120576 | bytes 1433600 | tf_op jit(solution)/shard_map/absorb/pallas_call | solution.py:79
  204.6 2.3 finish.1
  206.9 4.2 %all-to-all-start.1 = ((bf16[8,144,128]{2,1,0:T(8,128)(2,1)}), bf16[8,144,128]{2,1,0:T(8,128)(2,1)S(1)}, u32[]{:S(2)}, u32[]{:S(2)}) async-start(bf16[8,144,128]{2,1,0:T(8,128)(2,1)} %finish.1), calls=%async_computation.1 | async-start | bytes 589824 | tf_op jit(solution)/shard_map/all_to_all | solution.py:326
  211.8 10.2 %all-to-all-done.1.hidden_ref = bf16[8,144,128]{2,1,0:T(8,128)(2,1)S(1)} async-done(((bf16[8,144,128]{2,1,0:T(8,128)(2,1)}), bf16[8,144,128]{2,1,0:T(8,128)(2,1)S(1)}, u32[]{:S(2)}, u32[]{:S(2)}) %all-to-all-start.1) | async-done | bytes 294944 | tf_op jit(solution)/shard_map/all_to_all | solution.py:326
  222.7 3.8 %down.1 = bf16[144,896]{1,0:T(8,128)(2,1)} custom-call(s32[9]{0:T(128)} %concatenate.59.at_ref, bf16[8,144,128]{2,1,0:T(8,128)(2,1)} %copy-done.1, bf16[128,7168]{1,0:T(8,128)(2,1)} %bitcast.119, bf16[448,896]{1,0:T(8,128)(2,1)} %constant_dynamic-update-slice_fusion.5.mine_ref, bf16[448,896]{1,0:T(8,128)(2,1)} %collective-permute-done.19.other_ref), custom_call_target="tpu_custom_call" | custom-call | flops 264241152 | bytes 2129920 | tf_op jit(solution)/shard_map/down/pallas_call | solution.py:151
  226.5 1.8 reshape.236
  228.3 6.7 %all-to-all-start.2 = ((bf16[48,3,896]{2,1,0:T(4,128)(2,1)}), bf16[48,3,896]{2,1,0:T(4,128)(2,1)S(1)}, u32[]{:S(2)}, u32[]{:S(2)}) async-start(bf16[48,3,896]{2,1,0:T(4,128)(2,1)} %reshape.236), calls=%async_computation.2 | async-start | bytes 688128 | tf_op jit(solution)/shard_map/all_to_all | solution.py:334
  237.4 13.8 %all-to-all-done.2 = bf16[48,3,896]{2,1,0:T(4,128)(2,1)S(1)} async-done(((bf16[48,3,896]{2,1,0:T(4,128)(2,1)}), bf16[48,3,896]{2,1,0:T(4,128)(2,1)S(1)}, u32[]{:S(2)}, u32[]{:S(2)}) %all-to-all-start.2) | async-done | bytes 258080 | tf_op jit(solution)/shard_map/all_to_all | solution.py:334
  252.1 2.3 add_convert_fusion
  (90 shorter events, 28.2 us)
Async XLA Ops:
  0.6 85.3 %copy-start = (bf16[8,1,216,896]{3,2,1,0:T(8,128)(2,1)S(1)}, bf16[8,1,216,896]{3,2,1,0:T(8,128)(2,1)}, u32[]{:S(2)}) copy-start(bf16[8,1,216,896]{3,2,1,0:T(8,128)(2,1)} %param.15) | copy-start | bytes 9289732
  4.9 4.4 %collective-permute-start = (bf16[1,72,1152]{2,1,0:T(8,128)(2,1)S(1)}, bf16[1,72,1152]{2,1,0:T(8,128)(2,1)S(1)}, u32[]{:S(2)}, u32[]{:S(2)}) collective-permute-start(bf16[1,72,1152]{2,1,0:T(8,128)(2,1)S(1)} %get-tuple-element.42), channel_id=1, source_target_pairs={{0,1},{1,0},{2,3},{3,2},{4,5},{5,4},{6,7},{7,6},{8,9},{9,8},{10,11... | collective-permute-start | bytes 497672 | tf_op jit(solution)/shard_map/ppermute | solution.py:33
  9.2 34.6 %copy-start.6 = (s32[144]{0:T(256)}, s32[144]{0:T(256)S(1)}, u32[]{:S(2)}) copy-start(s32[144]{0:T(256)S(1)} %select_reduce_fusion) | copy-start | bytes 1732
  9.3 10.5 %collective-permute-start.1 = (bf16[2,72,1152]{2,1,0:T(8,128)(2,1)S(1)}, bf16[2,72,1152]{2,1,0:T(8,128)(2,1)S(1)}, u32[]{:S(2)}, u32[]{:S(2)}) collective-permute-start(bf16[2,72,1152]{2,1,0:T(8,128)(2,1)S(1)} %pad_maximum_fusion.1), channel_id=1, source_target_pairs={{0,96},{96,192},{192,288},{288,384},{384,480},{480,576},{576,672},... | collective-permute-start | bytes 995336 | tf_op jit(solution)/shard_map/ppermute | solution.py:40
  19.8 10.2 %collective-permute-start.2 = (bf16[2,72,1152]{2,1,0:T(8,128)(2,1)S(1)}, bf16[2,72,1152]{2,1,0:T(8,128)(2,1)S(1)}, u32[]{:S(2)}, u32[]{:S(2)}) collective-permute-start(bf16[2,72,1152]{2,1,0:T(8,128)(2,1)S(1)} %collective-permute-done.1), channel_id=1, source_target_pairs={{0,96},{96,192},{192,288},{288,384},{384,480},{480,576},{576,672},... | collective-permute-start | bytes 995336 | tf_op jit(solution)/shard_map/ppermute | solution.py:40
  30.0 10.2 %collective-permute-start.3 = (bf16[2,72,1152]{2,1,0:T(8,128)(2,1)S(1)}, bf16[2,72,1152]{2,1,0:T(8,128)(2,1)S(1)}, u32[]{:S(2)}, u32[]{:S(2)}) collective-permute-start(bf16[2,72,1152]{2,1,0:T(8,128)(2,1)S(1)} %collective-permute-done.2), channel_id=1, source_target_pairs={{0,96},{96,192},{192,288},{288,384},{384,480},{480,576},{576,672},... | collective-permute-start | bytes 995336 | tf_op jit(solution)/shard_map/ppermute | solution.py:40
  42.3 5.5 %copy-start.10 = (bf16[4608,216]{0,1:T(8,128)(2,1)S(1)}, bf16[4608,216]{0,1:T(8,128)(2,1)}, u32[]{:S(2)}) copy-start(bf16[4608,216]{0,1:T(8,128)(2,1)} %param.14) | copy-start | bytes 5971972
  44.0 13.1 %collective-permute-start.4 = (bf16[6,72,1152]{2,1,0:T(8,128)(2,1)S(1)}, bf16[6,72,1152]{2,1,0:T(8,128)(2,1)S(1)}, u32[]{:S(2)}, u32[]{:S(2)}) collective-permute-start(bf16[6,72,1152]{2,1,0:T(8,128)(2,1)S(1)} %pad_maximum_fusion), channel_id=1, source_target_pairs={{0,1},{1,0},{2,3},{3,2},{4,5},{5,4},{6,7},{7,6},{8,9},{9,8},{10,11... | collective-permute-start | bytes 2985992 | tf_op jit(solution)/shard_map/ppermute | solution.py:33
  45.9 10.2 %collective-permute-start.5 = (bf16[2,72,1152]{2,1,0:T(8,128)(2,1)S(1)}, bf16[2,72,1152]{2,1,0:T(8,128)(2,1)S(1)}, u32[]{:S(2)}, u32[]{:S(2)}) collective-permute-start(bf16[2,72,1152]{2,1,0:T(8,128)(2,1)S(1)} %collective-permute-done.3), channel_id=1, source_target_pairs={{0,96},{96,192},{192,288},{288,384},{384,480},{480,576},{576,672},... | collective-permute-start | bytes 995336 | tf_op jit(solution)/shard_map/ppermute | solution.py:40
  86.0 3.9 %copy-start.9 = (f32[144]{0:T(256)S(1)}, f32[144]{0:T(256)}, u32[]{:S(2)}) copy-start(f32[144]{0:T(256)} %get-tuple-element.44) | copy-start | bytes 1732
  87.1 8.2 %copy-start.3 = (bf16[256,896]{1,0:T(8,128)(2,1)}, bf16[256,896]{1,0:T(8,128)(2,1)S(1)}, u32[]{:S(2)}) copy-start(bf16[256,896]{1,0:T(8,128)(2,1)S(1)} %convolution_convert_fusion.1) | copy-start | bytes 1376260
  87.9 3.7 %collective-permute-start.6 = (bf16[128,896]{1,0:T(8,128)(2,1)}, bf16[128,896]{1,0:T(8,128)(2,1)}, u32[]{:S(2)}, u32[]{:S(2)}) collective-permute-start(bf16[128,896]{1,0:T(8,128)(2,1)} %dynamic-slice_bitcast_fusion.3), channel_id=1, source_target_pairs={{0,1},{1,0},{2,3},{3,2},{4,5},{5,4},{6,7},{7,6},{8,9},{9,8},{10,11... | collective-permute-start | bytes 688136 | tf_op jit(solution)/shard_map/ppermute | solution.py:33
  95.3 37.7 %all-to-all-start = ((bf16[48,3,896]{2,1,0:T(4,128)(2,1)}), bf16[48,3,896]{2,1,0:T(4,128)(2,1)S(1)}, u32[]{:S(2)}, u32[]{:S(2)}) async-start(bf16[48,3,896]{2,1,0:T(4,128)(2,1)} %reshape.234), calls=%async_computation | async-start | bytes 688128 | tf_op jit(solution)/shard_map/all_to_all | solution.py:308
  133.9 20.1 %collective-permute-start.11 = (bf16[144,896]{1,0:T(8,128)(2,1)}, bf16[144,896]{1,0:T(8,128)(2,1)S(1)}, u32[]{:S(2)}, u32[]{:S(2)}) collective-permute-start(bf16[144,896]{1,0:T(8,128)(2,1)} %reshape.235.refs_0_), channel_id=1, source_target_pairs={{0,672},{96,0},{192,96},{288,192},{384,288},{480,384},{576,480},{6... | collective-permute-start | bytes 774152 | tf_op jit(solution)/shard_map/ppermute | solution.py:29
  135.9 22.5 %collective-permute-start.7 = (bf16[144,896]{1,0:T(8,128)(2,1)}, bf16[144,896]{1,0:T(8,128)(2,1)}, u32[]{:S(2)}, u32[]{:S(2)}) collective-permute-start(bf16[144,896]{1,0:T(8,128)(2,1)} %reshape.235.refs_0_), channel_id=1, source_target_pairs={{0,96},{96,192},{192,288},{288,384},{384,480},{480,576},{576,672},... | collective-permute-start | bytes 774152 | tf_op jit(solution)/shard_map/ppermute | solution.py:29
  141.8 18.6 %collective-permute-start.15 = (bf16[128,896]{1,0:T(8,128)(2,1)}, bf16[128,896]{1,0:T(8,128)(2,1)}, u32[]{:S(2)}, u32[]{:S(2)}) collective-permute-start(bf16[128,896]{1,0:T(8,128)(2,1)} %get-tuple-element.6), channel_id=1, source_target_pairs={{0,96},{96,192},{192,288},{288,384},{384,480},{480,576},{576,672},... | collective-permute-start | bytes 688136 | tf_op jit(solution)/shard_map/ppermute | solution.py:40
  144.8 17.2 %collective-permute-start.16 = (bf16[128,896]{1,0:T(8,128)(2,1)}, bf16[128,896]{1,0:T(8,128)(2,1)S(1)}, u32[]{:S(2)}, u32[]{:S(2)}) collective-permute-start(bf16[128,896]{1,0:T(8,128)(2,1)} %get-tuple-element.7), channel_id=1, source_target_pairs={{0,192},{96,288},{192,384},{288,480},{384,576},{480,672},{576,0},{... | collective-permute-start | bytes 688136 | tf_op jit(solution)/shard_map/ppermute | solution.py:40
  150.7 17.3 %collective-permute-start.17 = (bf16[128,896]{1,0:T(8,128)(2,1)}, bf16[128,896]{1,0:T(8,128)(2,1)S(1)}, u32[]{:S(2)}, u32[]{:S(2)}) collective-permute-start(bf16[128,896]{1,0:T(8,128)(2,1)} %get-tuple-element.8), channel_id=1, source_target_pairs={{0,288},{96,384},{192,480},{288,576},{384,672},{480,0},{576,96},{6... | collective-permute-start | bytes 688136 | tf_op jit(solution)/shard_map/ppermute | solution.py:40
  154.1 18.8 %copy-start.4 = (bf16[144,896]{1,0:T(8,128)(2,1)}, bf16[144,896]{1,0:T(8,128)(2,1)S(1)}, u32[]{:S(2)}) copy-start(bf16[144,896]{1,0:T(8,128)(2,1)S(1)} %collective-permute-done.11.refs_1_) | copy-start | bytes 774148
  154.1 14.6 %collective-permute-start.12 = (bf16[144,896]{1,0:T(8,128)(2,1)S(1)}, bf16[144,896]{1,0:T(8,128)(2,1)}, u32[]{:S(2)}, u32[]{:S(2)}) collective-permute-start(bf16[144,896]{1,0:T(8,128)(2,1)S(1)} %collective-permute-done.11.refs_1_), channel_id=1, source_target_pairs={{0,672},{96,0},{192,96},{288,192},{384,288},{480,384},{576,480},{6... | collective-permute-start | bytes 774152 | tf_op jit(solution)/shard_map/ppermute | solution.py:29
  158.4 15.1 %collective-permute-start.8 = (bf16[144,896]{1,0:T(8,128)(2,1)}, bf16[144,896]{1,0:T(8,128)(2,1)}, u32[]{:S(2)}, u32[]{:S(2)}) collective-permute-start(bf16[144,896]{1,0:T(8,128)(2,1)} %collective-permute-done.7.refs_0_), channel_id=1, source_target_pairs={{0,96},{96,192},{192,288},{288,384},{384,480},{480,576},{576,672},... | collective-permute-start | bytes 774152 | tf_op jit(solution)/shard_map/ppermute | solution.py:29
  162.7 14.0 %collective-permute-start.18 = (bf16[64,896]{1,0:T(8,128)(2,1)S(1)}, bf16[64,896]{1,0:T(8,128)(2,1)S(1)}, u32[]{:S(2)}, u32[]{:S(2)}) collective-permute-start(bf16[64,896]{1,0:T(8,128)(2,1)S(1)} %dynamic-slice_bitcast_fusion.4), channel_id=1, source_target_pairs={{0,384},{96,480},{192,576},{288,672},{384,0},{480,96},{576,192},{6... | collective-permute-start | bytes 344072 | tf_op jit(solution)/shard_map/ppermute | solution.py:40
  168.7 16.4 %collective-permute-start.13 = (bf16[144,896]{1,0:T(8,128)(2,1)}, bf16[144,896]{1,0:T(8,128)(2,1)}, u32[]{:S(2)}, u32[]{:S(2)}) collective-permute-start(bf16[144,896]{1,0:T(8,128)(2,1)} %collective-permute-done.12.refs_1_), channel_id=1, source_target_pairs={{0,672},{96,0},{192,96},{288,192},{384,288},{480,384},{576,480},{6... | collective-permute-start | bytes 774152 | tf_op jit(solution)/shard_map/ppermute | solution.py:29
  173.6 9.6 %collective-permute-start.9 = (bf16[144,896]{1,0:T(8,128)(2,1)}, bf16[144,896]{1,0:T(8,128)(2,1)S(1)}, u32[]{:S(2)}, u32[]{:S(2)}) collective-permute-start(bf16[144,896]{1,0:T(8,128)(2,1)} %collective-permute-done.8.refs_0_), channel_id=1, source_target_pairs={{0,96},{96,192},{192,288},{288,384},{384,480},{480,576},{576,672},... | collective-permute-start | bytes 774152 | tf_op jit(solution)/shard_map/ppermute | solution.py:29
  177.4 34.3 %collective-permute-start.19 = (bf16[448,896]{1,0:T(8,128)(2,1)}, bf16[448,896]{1,0:T(8,128)(2,1)}, u32[]{:S(2)}, u32[]{:S(2)}) collective-permute-start(bf16[448,896]{1,0:T(8,128)(2,1)} %constant_dynamic-update-slice_fusion.5.mine_ref), channel_id=1, source_target_pairs={{0,1},{1,0},{2,3},{3,2},{4,5},{5,4},{6,7},{7,6},{8,9},{9,8},{10,11... | collective-permute-start | bytes 2408456 | tf_op jit(solution)/shard_map/ppermute | solution.py:33
  183.2 11.5 %copy-start.2 = (bf16[144,896]{1,0:T(8,128)(2,1)}, bf16[144,896]{1,0:T(8,128)(2,1)S(1)}, u32[]{:S(2)}) copy-start(bf16[144,896]{1,0:T(8,128)(2,1)S(1)} %collective-permute-done.9.refs_0_) | copy-start | bytes 774148
  183.2 21.4 %collective-permute-start.10 = (bf16[80,896]{1,0:T(8,128)(2,1)S(1)}, bf16[80,896]{1,0:T(8,128)(2,1)}, u32[]{:S(2)}, u32[]{:S(2)}) collective-permute-start(bf16[80,896]{1,0:T(8,128)(2,1)S(1)} %slice.132), channel_id=1, source_target_pairs={{0,96},{96,192},{192,288},{288,384},{384,480},{480,576},{576,672},... | collective-permute-start | bytes 430088 | tf_op jit(solution)/shard_map/ppermute | solution.py:29
  186.7 17.9 %collective-permute-start.14 = (bf16[64,896]{1,0:T(8,128)(2,1)}, bf16[64,896]{1,0:T(8,128)(2,1)}, u32[]{:S(2)}, u32[]{:S(2)}) collective-permute-start(bf16[64,896]{1,0:T(8,128)(2,1)} %slice.133), channel_id=1, source_target_pairs={{0,672},{96,0},{192,96},{288,192},{384,288},{480,384},{576,480},{6... | collective-permute-start | bytes 344072 | tf_op jit(solution)/shard_map/ppermute | solution.py:29
  206.9 15.0 %all-to-all-start.1 = ((bf16[8,144,128]{2,1,0:T(8,128)(2,1)}), bf16[8,144,128]{2,1,0:T(8,128)(2,1)S(1)}, u32[]{:S(2)}, u32[]{:S(2)}) async-start(bf16[8,144,128]{2,1,0:T(8,128)(2,1)} %finish.1), calls=%async_computation.1 | async-start | bytes 589824 | tf_op jit(solution)/shard_map/all_to_all | solution.py:326
  222.0 0.7 copy-start.1
  222.7 12.3 %copy-start.5 = (s32[128,8]{0,1:T(8,128)S(1)}, s32[128,8]{0,1:T(8,128)}, u32[]{:S(2)}) copy-start(s32[128,8]{0,1:T(8,128)} %param.16) | copy-start | bytes 12292
  222.7 12.3 %copy-start.7 = (s32[144]{0:T(256)S(1)}, s32[144]{0:T(256)}, u32[]{:S(2)}) copy-start(s32[144]{0:T(256)} %copy-done.6) | copy-start | bytes 1732
  222.7 12.3 %copy-start.8 = (f32[128,8]{0,1:T(8,128)S(1)}, f32[128,8]{0,1:T(8,128)}, u32[]{:S(2)}) copy-start(f32[128,8]{0,1:T(8,128)} %param.17) | copy-start | bytes 12292
  228.3 22.9 %all-to-all-start.2 = ((bf16[48,3,896]{2,1,0:T(4,128)(2,1)}), bf16[48,3,896]{2,1,0:T(4,128)(2,1)S(1)}, u32[]{:S(2)}, u32[]{:S(2)}) async-start(bf16[48,3,896]{2,1,0:T(4,128)(2,1)} %reshape.236), calls=%async_computation.2 | async-start | bytes 688128 | tf_op jit(solution)/shard_map/all_to_all | solution.py:334
